TPU v7x, 32 devices: a whole 2x2x4 slice. The times are simulated.
32 devices in a mesh: dp: 8 (over y, x, core), blk: 4 (over z).
Axes of the slice: x: 2, y: 2, z: 4, core: 2. Of those that a mesh axis runs over, the one named last changes fastest.
Arguments:
- tokens: bfloat16 [16, 2048, 768], P('dp', 'blk'), may hold values from -6 to 6
- cotangent: bfloat16 [16, 2048, 768], P('dp', 'blk'), may hold values from -6 to 6
- lengths: int32 [16], P('dp'), may hold values from 512 to 2048, as said below
- query_weight: bfloat16 [768, 768], P(('dp', 'blk')), may hold values from -0.21875 to 0.21875
- key_weight: bfloat16 [768, 768], P(('dp', 'blk')), may hold values from -0.21875 to 0.21875
- value_weight: bfloat16 [768, 768], P(('dp', 'blk')), may hold values from -0.21875 to 0.21875
- output_weight: bfloat16 [768, 768], P(('dp', 'blk')), may hold values from -1.75 to 1.75
- up_weight: bfloat16 [768, 3072], P(('dp', 'blk')), may hold values from -0.21875 to 0.21875
- down_weight: bfloat16 [3072, 768], P(('dp', 'blk')), may hold values from -0.109375 to 0.109375
- query_bias: bfloat16 [768], P(('dp', 'blk')), may hold values from -2 to 2
- value_bias: bfloat16 [768], P(('dp', 'blk')), may hold values from -2 to 2
- output_bias: bfloat16 [768], P(('dp', 'blk')), may hold values from -2 to 2
- up_bias: bfloat16 [3072], P(('dp', 'blk')), may hold values from -2 to 2
- down_bias: bfloat16 [768], P(('dp', 'blk')), may hold values from -2 to 2
- attn_gain: bfloat16 [768], P(('dp', 'blk')), may hold values from 0.5 to 1.5
- attn_shift: bfloat16 [768], P(('dp', 'blk')), may hold values from -2 to 2
- ffn_gain: bfloat16 [768], P(('dp', 'blk')), may hold values from 0.5 to 1.5
- ffn_shift: bfloat16 [768], P(('dp', 'blk')), may hold values from -2 to 2
Outputs:
- layer_out: bfloat16 [16, 2048, 768], P('dp', 'blk')
- tokens_grad: float32 [16, 2048, 768], P('dp', 'blk')
- grad_query_weight: float32 [768, 768], P(('dp', 'blk'))
- grad_key_weight: float32 [768, 768], P(('dp', 'blk'))
- grad_value_weight: float32 [768, 768], P(('dp', 'blk'))
- grad_output_weight: float32 [768, 768], P(('dp', 'blk'))
- grad_up_weight: float32 [768, 3072], P(('dp', 'blk'))
- grad_down_weight: float32 [3072, 768], P(('dp', 'blk'))
- grad_query_bias: float32 [768], P(('dp', 'blk'))
- grad_value_bias: float32 [768], P(('dp', 'blk'))
- grad_output_bias: float32 [768], P(('dp', 'blk'))
- grad_up_bias: float32 [3072], P(('dp', 'blk'))
- grad_down_bias: float32 [768], P(('dp', 'blk'))
- grad_attn_gain: float32 [768], P(('dp', 'blk'))
- grad_attn_shift: float32 [768], P(('dp', 'blk'))
- grad_ffn_gain: float32 [768], P(('dp', 'blk'))
- grad_ffn_shift: float32 [768], P(('dp', 'blk'))
Inputs may be any that keep to these rules, and one draw needn't show every extreme that they name: `lengths`: each sequence is valid up to its length; the first sequence of every data group of 2 has length exactly 2048; the others fall in buckets of at most 2048, 1536 or 1024 positions and hold at least half of their bucket.
All inputs are finite; a program needn't handle non-finite values.
Results may differ from a plain program's by a relative error of at most 0.018.
Values may be sent and summed in bfloat16 or wider, within the bound.
No kernel may reach another device: no remote copies, remote signals or barrier semaphores. Data moves between devices by JAX's collectives and lax.ppermute only.
A program may use at most 384 MiB of HBM per device.

v0:
```python
import functools

import jax
import jax.numpy as jnp
from jax import lax
from jax.experimental import pallas as pl
from jax.experimental.pallas import tpu as pltpu
from jax.sharding import Mesh
from jax.sharding import PartitionSpec as P

HEADS = 12
LANES = 128
PER_TILE = 2
SCORE_SCALE = 0.125 * 1.4426950408889634
MASKED = -1e30
ALL = ("pair", "core", "blk")
VMEM_LIMIT = 56 << 20


def shifted(array, axis, by):
    length = lax.axis_size(axis)
    return lax.ppermute(array, axis, [(i, (i + by) % length) for i in range(length)])


def matmul(left, right):
    return jnp.dot(left, right, preferred_element_type=jnp.float32)


def times_trans(left, right):
    return lax.dot_general(
        left, right, (((1,), (1,)), ((), ())), preferred_element_type=jnp.float32
    )


def trans_times(left, right):
    return lax.dot_general(
        left, right, (((0,), (0,)), ((), ())), preferred_element_type=jnp.float32
    )


def layer_norm(values, gain, shift):
    center = jnp.mean(values, axis=-1, keepdims=True)
    offset = values - center
    spread = jnp.mean(offset * offset, axis=-1, keepdims=True)
    return offset * lax.rsqrt(spread + 1e-12) * gain + shift


def gelu_tanh(values):
    return jax.nn.gelu(values, approximate=True)


def ring_body(
    tokens,
    cotangent,
    lengths,
    query_weight,
    key_weight,
    value_weight,
    output_weight,
    up_weight,
    down_weight,
    query_bias,
    value_bias,
    output_bias,
    up_bias,
    down_bias,
    attn_gain,
    attn_shift,
    ffn_gain,
    ffn_shift,
):
    seqs, stretch, width = tokens.shape
    rows = seqs * stretch
    heads = HEADS
    head = width // heads
    gathered = (
        lax.all_gather(query_weight, ("dp", "blk"), axis=0, tiled=True),
        lax.all_gather(key_weight, ("dp", "blk"), axis=0, tiled=True),
        lax.all_gather(value_weight, ("dp", "blk"), axis=0, tiled=True),
        lax.all_gather(output_weight, ("dp", "blk"), axis=0, tiled=True),
        lax.all_gather(up_weight, ("dp", "blk"), axis=0, tiled=True),
        lax.all_gather(down_weight, ("dp", "blk"), axis=0, tiled=True),
        lax.all_gather(query_bias, ("dp", "blk"), axis=0, tiled=True),
        lax.all_gather(value_bias, ("dp", "blk"), axis=0, tiled=True),
        lax.all_gather(output_bias, ("dp", "blk"), axis=0, tiled=True),
        lax.all_gather(up_bias, ("dp", "blk"), axis=0, tiled=True),
        lax.all_gather(down_bias, ("dp", "blk"), axis=0, tiled=True),
        lax.all_gather(attn_gain, ("dp", "blk"), axis=0, tiled=True),
        lax.all_gather(attn_shift, ("dp", "blk"), axis=0, tiled=True),
        lax.all_gather(ffn_gain, ("dp", "blk"), axis=0, tiled=True),
        lax.all_gather(ffn_shift, ("dp", "blk"), axis=0, tiled=True),
    )
    query_full, key_full, value_full, output_full, upper_full, lower_full = gathered[:6]
    (
        bias_query,
        bias_value,
        bias_output,
        bias_upper,
        bias_lower,
        gain_one,
        shift_one,
        gain_two,
        shift_two,
    ) = [item.astype(jnp.float32) for item in gathered[6:]]
    flat = tokens.reshape(rows, width)
    queries = (matmul(flat, query_full) + bias_query).astype(jnp.bfloat16)
    keys_own = matmul(flat, key_full).astype(jnp.bfloat16)
    values_own = (matmul(flat, value_full) + bias_value).astype(jnp.bfloat16)
    query_heads = queries.reshape(seqs, stretch, heads, head)
    own_block = lax.axis_index("blk")
    cycle_size = lax.axis_size("blk")
    start = jnp.int32(0)
    key_piece = lax.all_gather(keys_own.reshape(seqs, stretch, width), "blk", axis=1, tiled=True)
    value_piece = lax.all_gather(
        values_own.reshape(seqs, stretch, width), "blk", axis=1, tiled=True
    )
    count = key_piece.shape[1]
    span = min(count, stretch)
    row_max = jnp.full((seqs, stretch, heads), -1e30, jnp.float32)
    row_total = jnp.zeros((seqs, stretch, heads), jnp.float32)
    accum = jnp.zeros((seqs, stretch, heads, head), jnp.float32)
    for part_no in range(count // span):
        key_heads = key_piece[:, part_no * span : (part_no + 1) * span].reshape(
            seqs, span, heads, head
        )
        value_heads = value_piece[:, part_no * span : (part_no + 1) * span].reshape(
            seqs, span, heads, head
        )
        positions = start + part_no * span + jnp.arange(span, dtype=jnp.int32)
        valid = positions[None, :] < lengths[:, None]
        scores = (
            jnp.einsum(
                "sqhd,skhd->sqhk", query_heads, key_heads, preferred_element_type=jnp.float32
            )
            * 0.125
        )
        scores = jnp.where(valid[:, None, None, :], scores, -jnp.inf)
        new_max = jnp.maximum(row_max, jnp.max(scores, axis=-1))
        expo = jnp.exp(scores - new_max[..., None])
        factor = jnp.exp(row_max - new_max)
        row_total = row_total * factor + jnp.sum(expo, axis=-1)
        accum = accum * factor[..., None] + jnp.einsum(
            "sqhk,skhd->sqhd",
            expo.astype(jnp.bfloat16),
            value_heads,
            preferred_element_type=jnp.float32,
        )
        row_max = new_max
    row_max, row_total, accum = (row_max, row_total, accum)
    log_total = row_max + jnp.log(row_total)
    context_full = accum / row_total[..., None]
    context = context_full.reshape(rows, width).astype(jnp.bfloat16)
    attended = matmul(context, output_full) + bias_output
    hidden, norm_one_back = jax.vjp(
        layer_norm, flat.astype(jnp.float32) + attended, gain_one, shift_one
    )
    hidden_low = hidden.astype(jnp.bfloat16)
    upward = matmul(hidden_low, upper_full) + bias_upper
    active_full, gelu_back = jax.vjp(gelu_tanh, upward)
    active = active_full.astype(jnp.bfloat16)
    downward = matmul(active, lower_full) + bias_lower
    output_full32, norm_two_back = jax.vjp(layer_norm, hidden + downward, gain_two, shift_two)
    layer_out = output_full32.astype(jnp.bfloat16).reshape(seqs, stretch, width)
    query_back, key_back, value_back, output_back, upper_back, lower_back = (
        lax.all_gather(query_weight, ("dp", "blk"), axis=0, tiled=True),
        lax.all_gather(key_weight, ("dp", "blk"), axis=0, tiled=True),
        lax.all_gather(value_weight, ("dp", "blk"), axis=0, tiled=True),
        lax.all_gather(output_weight, ("dp", "blk"), axis=0, tiled=True),
        lax.all_gather(up_weight, ("dp", "blk"), axis=0, tiled=True),
        lax.all_gather(down_weight, ("dp", "blk"), axis=0, tiled=True),
    )
    grad_outer = cotangent.reshape(rows, width).astype(jnp.float32)
    grad_res_two, grad_gain_two, grad_shift_two = norm_two_back(grad_outer)
    grad_down = grad_res_two.astype(jnp.bfloat16)
    grad_lower_bias = jnp.sum(grad_down, axis=0, dtype=jnp.float32)
    grad_lower = trans_times(active, grad_down)
    grad_active = times_trans(grad_down, lower_back)
    (grad_upward,) = gelu_back(grad_active)
    grad_up = grad_upward.astype(jnp.bfloat16)
    grad_upper_bias = jnp.sum(grad_up, axis=0, dtype=jnp.float32)
    grad_upper = trans_times(hidden_low, grad_up)
    grad_hidden = grad_res_two + times_trans(grad_up, upper_back)
    grad_res_one, grad_gain_one, grad_shift_one = norm_one_back(grad_hidden)
    grad_attended = grad_res_one.astype(jnp.bfloat16)
    grad_output_bias = jnp.sum(grad_attended, axis=0, dtype=jnp.float32)
    grad_output = trans_times(context, grad_attended)
    grad_context = times_trans(grad_attended, output_back).astype(jnp.bfloat16)
    context_grad_heads = grad_context.reshape(seqs, stretch, heads, head)
    delta = jnp.sum(context_grad_heads.astype(jnp.float32) * context_full, axis=-1)

    def contribute(key_value, source, pair_grad, query_grad):
        key_heads = key_value[0]
        value_heads = key_value[1]
        positions = source * stretch + jnp.arange(stretch, dtype=jnp.int32)
        valid = positions[None, :] < lengths[:, None]
        scores = (
            jnp.einsum(
                "sqhd,skhd->sqhk", query_heads, key_heads, preferred_element_type=jnp.float32
            )
            * 0.125
        )
        probs = jnp.where(valid[:, None, None, :], jnp.exp(scores - log_total[..., None]), 0.0)
        grad_probs = jnp.einsum(
            "sqhd,skhd->sqhk", context_grad_heads, value_heads, preferred_element_type=jnp.float32
        )
        grad_scores = (probs * (grad_probs - delta[..., None])).astype(jnp.bfloat16)
        query_grad = (
            query_grad
            + jnp.einsum(
                "sqhk,skhd->sqhd", grad_scores, key_heads, preferred_element_type=jnp.float32
            )
            * 0.125
        )
        key_part = (
            jnp.einsum(
                "sqhk,sqhd->skhd", grad_scores, query_heads, preferred_element_type=jnp.float32
            )
            * 0.125
        )
        value_part = jnp.einsum(
            "sqhk,sqhd->skhd",
            probs.astype(jnp.bfloat16),
            context_grad_heads,
            preferred_element_type=jnp.float32,
        )
        pair_grad = pair_grad + jnp.stack([key_part, value_part])
        return (pair_grad, query_grad)

    def rotate_grads(pair_grad):
        return shifted(pair_grad.astype(jnp.bfloat16), "blk", 1).astype(pair_grad.dtype)

    key_value_own = jnp.stack(
        [
            keys_own.reshape(seqs, stretch, heads, head),
            values_own.reshape(seqs, stretch, heads, head),
        ]
    )
    pair_grad, query_grad = contribute(
        key_value_own,
        own_block,
        jnp.zeros((2, seqs, stretch, heads, head), jnp.float32),
        jnp.zeros((seqs, stretch, heads, head), jnp.float32),
    )

    def cycle_turn(turn, state):
        key_value_now, pair_now, query_now = state
        key_value_now = shifted(key_value_now, "blk", 1)
        pair_now = rotate_grads(pair_now)
        source = (own_block - turn) % cycle_size
        pair_now, query_now = contribute(key_value_now, source, pair_now, query_now)
        return (key_value_now, pair_now, query_now)

    final_state = lax.fori_loop(1, cycle_size, cycle_turn, (key_value_own, pair_grad, query_grad))
    pair_home = rotate_grads(final_state[1])
    grad_queries = final_state[2].reshape(rows, width).astype(jnp.bfloat16)
    grad_keys = pair_home[0].reshape(rows, width).astype(jnp.bfloat16)
    grad_values = pair_home[1].reshape(rows, width).astype(jnp.bfloat16)
    grad_query = trans_times(flat, grad_queries)
    grad_key = trans_times(flat, grad_keys)
    grad_value = trans_times(flat, grad_values)
    grad_query_bias = jnp.sum(grad_queries, axis=0, dtype=jnp.float32)
    grad_value_bias = jnp.sum(grad_values, axis=0, dtype=jnp.float32)
    tokens_grad = (
        grad_res_one
        + times_trans(grad_queries, query_back)
        + times_trans(grad_keys, key_back)
        + times_trans(grad_values, value_back)
    ).reshape(seqs, stretch, width)
    shares = (
        lax.psum_scatter(grad_query, ("dp", "blk"), scatter_dimension=0, tiled=True),
        lax.psum_scatter(grad_key, ("dp", "blk"), scatter_dimension=0, tiled=True),
        lax.psum_scatter(grad_value, ("dp", "blk"), scatter_dimension=0, tiled=True),
        lax.psum_scatter(grad_output, ("dp", "blk"), scatter_dimension=0, tiled=True),
        lax.psum_scatter(grad_upper, ("dp", "blk"), scatter_dimension=0, tiled=True),
        lax.psum_scatter(grad_lower, ("dp", "blk"), scatter_dimension=0, tiled=True),
        lax.psum_scatter(grad_query_bias, ("dp", "blk"), scatter_dimension=0, tiled=True),
        lax.psum_scatter(grad_value_bias, ("dp", "blk"), scatter_dimension=0, tiled=True),
        lax.psum_scatter(grad_output_bias, ("dp", "blk"), scatter_dimension=0, tiled=True),
        lax.psum_scatter(grad_upper_bias, ("dp", "blk"), scatter_dimension=0, tiled=True),
        lax.psum_scatter(grad_lower_bias, ("dp", "blk"), scatter_dimension=0, tiled=True),
        lax.psum_scatter(grad_gain_one, ("dp", "blk"), scatter_dimension=0, tiled=True),
        lax.psum_scatter(grad_shift_one, ("dp", "blk"), scatter_dimension=0, tiled=True),
        lax.psum_scatter(grad_gain_two, ("dp", "blk"), scatter_dimension=0, tiled=True),
        lax.psum_scatter(grad_shift_two, ("dp", "blk"), scatter_dimension=0, tiled=True),
    )
    return (layer_out, tokens_grad) + tuple(shares)


def dot_f32(left, right, dims):
    return lax.dot_general(left, right, (dims, ((), ())), preferred_element_type=jnp.float32)


NT = ((1,), (1,))
NN = ((1,), (0,))


def split_three(values):
    high = values.astype(jnp.bfloat16).astype(jnp.float32)
    rest = values - high
    mid = rest.astype(jnp.bfloat16).astype(jnp.float32)
    return high, mid, rest - mid


def spread_three(lane, base, values, into):
    for step, part in enumerate(split_three(values)):
        into = jnp.where(lane == base + step, part, into)
    return into


def fill_keys(info_ref, keys, values, key_aug, value_aug, value_fill, chunk):
    length = keys.shape[0]
    lane = lax.broadcasted_iota(jnp.int32, (chunk, LANES), 1)
    row = lax.broadcasted_iota(jnp.int32, (chunk, LANES), 0)
    for part in range(length // chunk):
        at = slice(part * chunk, (part + 1) * chunk)
        off = (lane == 3) & (row + info_ref[1 + part] >= info_ref[0])
        mask = jnp.where(off, MASKED, 0.0)
        for one in range(PER_TILE):
            mine = lane // (LANES // PER_TILE) == one
            base = 4 * one
            minus = (lane >= base) & (lane < base + 3)
            key_aug[one, at, :LANES] = jnp.where(mine, keys[at], jnp.zeros((), keys.dtype))
            key_aug[one, at, LANES:] = jnp.where(minus, -1.0, mask).astype(jnp.bfloat16)
            value_aug[one, at, :LANES] = jnp.where(mine, values[at], jnp.zeros((), keys.dtype))
            if value_fill:
                value_aug[one, at, LANES:] = jnp.ones((chunk, LANES), jnp.bfloat16)
            else:
                value_aug[one, at, LANES:] = jnp.where(minus, -1.0, 0.0).astype(jnp.bfloat16)


def attend_kernel(
    span, info_ref, query_ref, key_ref, value_ref, near_ref, far_ref, out_ref, aux_ref, key_aug, value_aug
):
    length = key_ref.shape[0]
    tile = query_ref.shape[0]
    lane = lax.broadcasted_iota(jnp.int32, (1, LANES), 1)

    fill_keys(info_ref, key_ref, value_ref, key_aug, value_aug, True, length // 8)

    one_lane = jnp.where(lane == 3, 1.0, 0.0)
    flag = jnp.broadcast_to(one_lane.astype(jnp.bfloat16), (tile, LANES))
    query = jnp.concatenate([query_ref[...], flag], axis=1)
    pieces = [slice(at, at + span) for at in range(0, length, span)]
    scores, peaks = [], []
    for one in range(PER_TILE):
        peak = None
        row = []
        for at in pieces:
            score = dot_f32(query, key_aug[one, at], NT)
            row.append(score)
            for low in range(0, span, LANES):
                part = score[:, low : low + LANES]
                peak = part if peak is None else jnp.maximum(peak, part)
        scores.append(row)
        peaks.append(jnp.max(peak, axis=1, keepdims=True))
    out = None
    aux = one_lane
    for one in range(PER_TILE):
        total = None
        for at, score in zip(pieces, scores[one]):
            expo = jnp.exp2((score - peaks[one]) * SCORE_SCALE).astype(jnp.bfloat16)
            part = dot_f32(expo, value_aug[one, at], NN)
            total = part if total is None else total + part
        weight = total[:, LANES:]
        part = total[:, :LANES] / weight
        out = part if out is None else out + part
        log_total = jnp.log2(weight) * (1.0 / SCORE_SCALE) + peaks[one]
        aux = spread_three(lane, 4 * one, log_total, aux)
    low = out.astype(jnp.bfloat16)
    near_ref[...] = low[: tile // 2]
    far_ref[...] = low[tile // 2 :]
    out_ref[...] = out
    aux_ref[...] = aux.astype(jnp.bfloat16)


def attend(qkv, info, part, parts, span):
    length, width = qkv.shape[0], qkv.shape[1] // 3
    tiles, rows = width // LANES, length // parts
    half = pl.BlockSpec((rows // 2, LANES), lambda pair: (0, pair))
    whole = pl.BlockSpec((rows, LANES), lambda pair: (0, pair))
    block = jax.ShapeDtypeStruct((rows // 2, width), jnp.bfloat16)
    return pl.pallas_call(
        functools.partial(attend_kernel, span),
        grid=(tiles,),
        in_specs=[
            pl.BlockSpec(memory_space=pltpu.SMEM),
            pl.BlockSpec((rows, LANES), lambda pair: (part, pair)),
            pl.BlockSpec((length, LANES), lambda pair: (0, tiles + pair)),
            pl.BlockSpec((length, LANES), lambda pair: (0, 2 * tiles + pair)),
        ],
        out_specs=[half, half, whole, whole],
        out_shape=[
            block,
            block,
            jax.ShapeDtypeStruct((rows, width), jnp.float32),
            jax.ShapeDtypeStruct((rows, width), jnp.bfloat16),
        ],
        scratch_shapes=[pltpu.VMEM((PER_TILE, length, 2 * LANES), jnp.bfloat16)] * 2,
        compiler_params=pltpu.CompilerParams(vmem_limit_bytes=VMEM_LIMIT),
        cost_estimate=pl.CostEstimate(
            flops=16 * rows * length * width,
            bytes_accessed=12 * length * width,
            transcendentals=rows * length * width // 64,
        ),
        name="attend",
    )(info, qkv, qkv, qkv)


def attend_back_kernel(span, counts, info_ref, query_ref, key_ref, value_ref, *refs):
    groups = []
    for count in counts:
        groups.append(refs[:count])
        refs = refs[count:]
    query_grad_ref, key_grad_ref, value_grad_ref, key_aug, value_aug, key_cols, key_sum, value_sum = refs
    length = key_ref.shape[0]
    tile = query_ref.shape[0]
    wide = LANES // PER_TILE
    lane = lax.broadcasted_iota(jnp.int32, (1, LANES), 1)
    step = pl.program_id(1)

    @pl.when(step == 0)
    def _():
        fill_keys(info_ref, key_ref, value_ref, key_aug, value_aug, False, length // 8)
        key_cols[...] = key_ref[...].T
        key_sum[...] = jnp.zeros_like(key_sum)
        value_sum[...] = jnp.zeros_like(value_sum)

    taken = []
    for group in groups:
        per_piece = length // len(group) // tile
        item = group[0][...]
        for at in range(1, len(group)):
            item = jnp.where(step >= at * per_piece, group[at][...], item)
        taken.append(item)
    grad, out, aux = taken
    plain = query_ref[...]
    query = jnp.concatenate([plain, aux], axis=1)
    product = grad.astype(jnp.float32) * out
    delta = jnp.zeros((tile, LANES), jnp.float32)
    for one in range(PER_TILE):
        own = jnp.sum(jnp.where(lane // wide == one, product, 0.0), axis=1, keepdims=True)
        delta = spread_three(lane, 4 * one, own, delta)
    grad_aug = jnp.concatenate([grad, delta.astype(jnp.bfloat16)], axis=1)
    nothing = jnp.zeros((), plain.dtype)
    query_rows = []
    for one in range(PER_TILE):
        mine = lane // wide == one
        query_own = jnp.where(mine, plain, nothing)
        grad_own = jnp.where(mine, grad, nothing)
        total = None
        for low in range(0, length, span):
            at = slice(low, low + span)
            score = dot_f32(key_aug[one, at], query, NT)
            grad_probs = dot_f32(value_aug[one, at], grad_aug, NT)
            probs = jnp.exp2(score * SCORE_SCALE)
            grad_scores = (probs * grad_probs).astype(jnp.bfloat16)
            value_sum[at] += dot_f32(probs.astype(jnp.bfloat16), grad_own, NN)
            key_sum[at] += dot_f32(grad_scores, query_own, NN)
            part = dot_f32(key_cols[wide * one : wide * (one + 1), at], grad_scores, NN)
            total = part if total is None else total + part
        query_rows.append(total)
    query_grad_ref[...] = (jnp.concatenate(query_rows, axis=0).T * 0.125).astype(jnp.bfloat16)

    @pl.when(step == pl.num_programs(1) - 1)
    def _():
        key_grad_ref[...] = (key_sum[...] * 0.125).astype(jnp.bfloat16)
        value_grad_ref[...] = value_sum[...].astype(jnp.bfloat16)


def attend_back(qkv, grads, outs, auxes, info, tile, span):
    length, width = qkv.shape[0], qkv.shape[1] // 3
    tiles = width // LANES

    def piece_specs(pieces):
        per_piece = length // len(pieces) // tile
        return [
            pl.BlockSpec(
                (tile, LANES),
                lambda pair, at, low=low: (jnp.clip(at - low, 0, per_piece - 1), pair),
            )
            for low in range(0, per_piece * len(pieces), per_piece)
        ]

    result = jax.ShapeDtypeStruct((length, width), jnp.bfloat16)
    whole = pl.BlockSpec((length, LANES), lambda pair, at: (0, pair))
    query_spec = pl.BlockSpec((tile, LANES), lambda pair, at: (at, pair))
    return pl.pallas_call(
        functools.partial(attend_back_kernel, span, (len(grads), len(outs), len(auxes))),
        grid=(tiles, length // tile),
        in_specs=[
            pl.BlockSpec(memory_space=pltpu.SMEM),
            query_spec,
            pl.BlockSpec((length, LANES), lambda pair, at: (0, tiles + pair)),
            pl.BlockSpec((length, LANES), lambda pair, at: (0, 2 * tiles + pair)),
        ]
        + piece_specs(grads)
        + piece_specs(outs)
        + piece_specs(auxes),
        out_specs=[query_spec, whole, whole],
        out_shape=[result] * 3,
        scratch_shapes=[pltpu.VMEM((PER_TILE, length, 2 * LANES), jnp.bfloat16)] * 2
        + [pltpu.VMEM((LANES, length), jnp.bfloat16)]
        + [pltpu.VMEM((length, LANES), jnp.float32)] * 2,
        compiler_params=pltpu.CompilerParams(vmem_limit_bytes=VMEM_LIMIT),
        cost_estimate=pl.CostEstimate(
            flops=40 * length * length * width,
            bytes_accessed=22 * length * width,
            transcendentals=length * length * width // 64,
        ),
        name="attend_back",
    )(info, qkv, qkv, qkv, *grads, *outs, *auxes)


def pack_kernel(count, core_ref, *refs):
    query, key, value, output, up, down = refs[:6]
    vectors = refs[6 : 6 + count]
    mine_ref, theirs_ref, second_ref, held_ref, wide_ref = refs[6 + count : 11 + count]
    lines = refs[11 + count : 11 + 2 * count]
    sems, line_sems = refs[11 + 2 * count :]
    share, width = query.shape
    cols = width // 2
    fold = up.shape[1] // width
    copies = [
        pltpu.make_async_copy(item, held_ref.at[at], sems.at[at])
        for at, item in enumerate((query, key, value))
    ]
    copies += [
        pltpu.make_async_copy(item, line, line_sems.at[at])
        for at, (item, line) in enumerate(zip(vectors, lines))
    ]
    later = [pltpu.make_async_copy(output, second_ref.at[0], sems.at[3])]
    for at in range(fold):
        later.append(
            pltpu.make_async_copy(
                down.at[pl.ds(at * share, share)],
                second_ref.at[1 + fold + at],
                sems.at[4 + at],
            )
        )
    later.append(pltpu.make_async_copy(up, wide_ref, sems.at[4 + fold]))
    for copy in copies + later:
        copy.start()
    for copy in copies:
        copy.wait()
    first_core = core_ref[0] == 0
    for at in range(3):
        left, right = held_ref[at, :, :cols], held_ref[at, :, cols:]
        here = slice(at * share, (at + 1) * share)
        mine_ref[here] = jnp.where(first_core, left, right)
        theirs_ref[here] = jnp.where(first_core, right, left)
    for ref in (mine_ref, theirs_ref):
        ref[3 * share :] = jnp.zeros((8, cols), ref.dtype)
        for at, line in enumerate(lines):
            low = at // 8 * LANES
            ref[3 * share + at % 8, low : low + line.shape[0]] = line[...]
    for copy in later:
        copy.wait()
    for at in range(fold):
        second_ref[1 + at] = wide_ref[:, at * width : (at + 1) * width]


def pack(core, matrices, vectors):
    share, width = matrices[0].shape
    cols = width // 2
    fold = matrices[4].shape[1] // width
    count = len(vectors)
    block = jax.ShapeDtypeStruct((3 * share + 8, cols), jnp.bfloat16)
    inside = pl.BlockSpec(memory_space=pltpu.VMEM)
    return pl.pallas_call(
        functools.partial(pack_kernel, count),
        in_specs=[pl.BlockSpec(memory_space=pltpu.SMEM)]
        + [pl.BlockSpec(memory_space=pl.ANY)] * (6 + count),
        out_specs=[inside] * 3,
        out_shape=[
            block,
            block,
            jax.ShapeDtypeStruct((1 + 2 * fold, share, width), jnp.bfloat16),
        ],
        scratch_shapes=[pltpu.VMEM((3, share, width), jnp.bfloat16)]
        + [pltpu.VMEM(matrices[4].shape, jnp.bfloat16)]
        + [pltpu.VMEM(item.shape, item.dtype) for item in vectors]
        + [pltpu.SemaphoreType.DMA((5 + fold,)), pltpu.SemaphoreType.DMA((count,))],
        compiler_params=pltpu.CompilerParams(vmem_limit_bytes=VMEM_LIMIT),
        name="pack",
    )(core, *matrices, *vectors)


def by_device(gathered_ref, rows, columns=slice(None)):
    n_pair, n_blk, n_core = gathered_ref.shape[:3]
    return jnp.concatenate(
        [
            gathered_ref[pair, blk, core, rows, columns]
            for pair in range(n_pair)
            for core in range(n_core)
            for blk in range(n_blk)
        ],
        axis=0,
    )


def unspread(gathered_ref, first_row, entry, width, share):
    low, row = entry // 8 * LANES, first_row + entry % 8
    pieces = by_device(gathered_ref, slice(row, row + 1), slice(low, low + LANES))
    lane = lax.broadcasted_iota(jnp.int32, (LANES, width), 1)
    row = lax.broadcasted_iota(jnp.int32, (LANES, width), 0)
    pick = jnp.where(lax.rem(lane, share) == row, 1.0, 0.0).astype(jnp.bfloat16)
    spread = dot_f32(pieces, pick, NN)
    lane = lax.broadcasted_iota(jnp.int32, (pieces.shape[0], width), 1)
    row = lax.broadcasted_iota(jnp.int32, (pieces.shape[0], width), 0)
    return jnp.sum(jnp.where(lax.div(lane, share) == row, spread, 0.0), axis=0, keepdims=True)


def own_weight(gathered_ref, at, share):
    return by_device(gathered_ref, slice(at * share, (at + 1) * share))


def block_rows(core_ref, own_ref, other_ref):
    own, other = own_ref[...], other_ref[...]
    first = core_ref[0] == 0
    return jnp.concatenate([jnp.where(first, own, other), jnp.where(first, other, own)], axis=0)


def block_specs(half, width):
    return [
        pl.BlockSpec((half, width), lambda at, core: (at, 0)),
        pl.BlockSpec((half, width), lambda at, core: (at + 1 - 2 * lax.rem(at, 2), 0)),
    ]


def project_kernel(share, core_ref, own_ref, other_ref, gathered_ref, out_ref, bias_ref):
    cols = gathered_ref.shape[4]

    @pl.when(pl.program_id(0) == 0)
    def _():
        for at in range(2):
            whole = unspread(gathered_ref, 3 * share, at, 2 * cols, share)
            bias_ref[at : at + 1, :] = jnp.where(
                core_ref[0] == 0, whole[:, :cols], whole[:, cols:]
            )

    tokens = block_rows(core_ref, own_ref, other_ref)
    for at, bias in enumerate((0, None, 1)):
        part = dot_f32(tokens, own_weight(gathered_ref, at, share), NN)
        if bias is not None:
            part = part + bias_ref[bias : bias + 1, :]
        out_ref[:, at * cols : (at + 1) * cols] = part.astype(out_ref.dtype)


def project(core, own, other, gathered, half):
    length, width = 2 * own.shape[0], own.shape[1]
    cols, share = width // 2, (gathered.shape[3] - 8) // 3
    return pl.pallas_call(
        functools.partial(project_kernel, share),
        grid_spec=pltpu.PrefetchScalarGridSpec(
            num_scalar_prefetch=1,
            grid=(length // (2 * half),),
            in_specs=block_specs(half, width)
            + [pl.BlockSpec(gathered.shape, lambda at, core: (0,) * 5)],
            out_specs=pl.BlockSpec((2 * half, 3 * cols), lambda at, core: (at, 0)),
            scratch_shapes=[pltpu.VMEM((8, cols), jnp.float32)],
        ),
        out_shape=jax.ShapeDtypeStruct((length, 3 * cols), jnp.bfloat16),
        compiler_params=pltpu.CompilerParams(vmem_limit_bytes=VMEM_LIMIT),
        cost_estimate=pl.CostEstimate(
            flops=6 * length * width * cols, bytes_accessed=10 * length * width, transcendentals=0
        ),
        name="project",
    )(core, own, other, gathered)


def norm(values, gain, shift):
    center = jnp.mean(values, axis=1, keepdims=True)
    offset = values - center
    scale = lax.rsqrt(jnp.mean(offset * offset, axis=1, keepdims=True) + 1e-12)
    unit = offset * scale
    return unit * gain + shift, unit, scale


def norm_back(grad, gain, unit, scale):
    inner = grad * gain
    mean = jnp.mean(inner, axis=1, keepdims=True)
    return scale * (inner - mean - unit * jnp.mean(inner * unit, axis=1, keepdims=True))


def feed_kernel(
    kept, index_ref, even_ref, odd_ref, tokens_ref, cotangent_ref, small_ref, weights_ref, *refs
):
    feed_rows(
        index_ref[1] == 1, even_ref, odd_ref, tokens_ref, cotangent_ref, small_ref, weights_ref, *refs[kept:]
    )


def feed_rows(
    odd, even_ref, odd_ref, tokens_ref, cotangent_ref, small_ref, weights_ref,
    out_ref, active_ref, grad_down_ref, grad_up_ref, hidden_ref, res_ref, attended_ref, context_ref,
    even_grad_ref, odd_grad_ref, sum_ref,
    weight_ref, vector_ref, slope_ref, sems,
):
    devices, _, share, width = weights_ref.shape
    fold = active_ref.shape[1] // width
    group = devices // fold
    step = pl.program_id(0)
    f32, bf16 = jnp.float32, jnp.bfloat16

    def copy(unit):
        if unit <= fold:
            return pltpu.make_async_copy(weights_ref.at[:, unit], weight_ref.at[unit], sems.at[unit])
        first = group * (unit - 1 - fold)
        return pltpu.make_async_copy(
            weights_ref.at[pl.ds(first, group), pl.ds(1 + fold, fold)],
            weight_ref.at[unit].reshape(group, fold, share, width),
            sems.at[unit],
        )

    order = [0]
    for at in range(fold):
        order += [1 + at, 1 + fold + at]
    ahead = 3

    @pl.when(step == 0)
    def _():
        for unit in order[:ahead]:
            copy(unit).start()
        sum_ref[...] = jnp.zeros_like(sum_ref)
        for entry in range(7):
            times = fold if entry == 1 else 1
            vector_ref[entry : entry + 1, : times * width] = unspread(
                small_ref, 0, 2 + entry, times * width, times * share
            )

    def ready(unit):
        @pl.when(step == 0)
        def _():
            copy(unit).wait()
            after = order.index(unit) + ahead
            if after < len(order):
                copy(order[after]).start()

    def weight(unit):
        return weight_ref[unit].reshape(width, width)

    def vector(entry, low=0):
        return vector_ref[entry : entry + 1, low : low + width]

    def add_sum(entry, value):
        sum_ref[entry : entry + 1, :] += jnp.sum(value, axis=0, keepdims=True)

    even, other = even_ref[...], odd_ref[...]
    context = jnp.concatenate([jnp.where(odd, other, even), jnp.where(odd, even, other)], axis=1)
    context_ref[...] = context
    ready(0)
    attended = dot_f32(context, weight(0), NN) + vector(0)
    hidden, unit_one, scale_one = norm(tokens_ref[...].astype(f32) + attended, vector(3), vector(4))
    hidden_low = hidden.astype(bf16)
    hidden_ref[...] = hidden_low
    down = vector(2)
    for at in range(fold):
        low = at * width
        ready(1 + at)
        up = dot_f32(hidden_low, weight(1 + at), NN) + vector(1, low)
        square = up * up
        tanh = jnp.tanh(0.7978845608 * up * (1.0 + 0.044715 * square))
        half = 0.5 * (1.0 + tanh)
        active = (up * half).astype(bf16)
        rise = (0.5 * 0.7978845608) * up * (1.0 - tanh * tanh)
        slope_ref[at] = half + rise * (1.0 + (3 * 0.044715) * square)
        active_ref[:, low : low + width] = active
        ready(1 + fold + at)
        down = down + dot_f32(active, weight(1 + fold + at), NN)
    out, unit_two, scale_two = norm(hidden + down, vector(5), vector(6))
    out_ref[...] = out.astype(bf16)
    cotangent = cotangent_ref[...].astype(f32)
    add_sum(4, cotangent * unit_two)
    add_sum(5, cotangent)
    grad = norm_back(cotangent, vector(5), unit_two, scale_two)
    grad_down = grad.astype(bf16)
    grad_down_ref[...] = grad_down
    add_sum(1, grad_down.astype(f32))
    for at in range(fold):
        low = at * width
        grad_active = dot_f32(grad_down, weight(1 + fold + at), NT)
        grad_up = (grad_active * slope_ref[at]).astype(bf16)
        grad_up_ref[:, low : low + width] = grad_up
        add_sum(6 + at, grad_up.astype(f32))
        grad = grad + dot_f32(grad_up, weight(1 + at), NT)
    add_sum(2, grad * unit_one)
    add_sum(3, grad)
    res_one = norm_back(grad, vector(3), unit_one, scale_one)
    res_ref[...] = res_one
    grad_attended = res_one.astype(bf16)
    attended_ref[...] = grad_attended
    add_sum(0, grad_attended.astype(f32))
    context_grad = dot_f32(grad_attended, weight(0), NT).astype(bf16)
    left, right = context_grad[:, : width // 2], context_grad[:, width // 2 :]
    even_grad_ref[...] = jnp.where(odd, right, left)
    odd_grad_ref[...] = jnp.where(odd, left, right)


def feed(index, even, other, tokens, cotangent, gathered, second, kept, tile):
    rows, width = even.shape[0], 2 * even.shape[1]
    seqs = tokens.shape[0]
    devices, units, share, _ = second.shape
    fold = (units - 1) // 2
    thin = pl.BlockSpec((tile, width), lambda at, index: (at, 0))
    placed = pl.BlockSpec((None, tile, width), lambda at, index: (index[0], at, 0))
    side = pl.BlockSpec((tile, width // 2), lambda at, index: (at, 0))
    wide = pl.BlockSpec((tile, fold * width), lambda at, index: (at, 0))
    sums = (6 + fold + 7) // 8 * 8

    def like(columns, dtype):
        return jax.ShapeDtypeStruct((rows, columns), dtype)

    bf16, f32 = jnp.bfloat16, jnp.float32
    return pl.pallas_call(
        functools.partial(feed_kernel, len(kept)),
        grid_spec=pltpu.PrefetchScalarGridSpec(
            num_scalar_prefetch=1,
            grid=(rows // tile,),
            in_specs=[
                side,
                side,
                placed,
                placed,
                pl.BlockSpec(
                    gathered.shape[:3] + (8, width // 2),
                    lambda at, index: (0, 0, 0, 3 * share // 8, 0),
                ),
                pl.BlockSpec(memory_space=pl.ANY),
            ]
            + [pl.BlockSpec(memory_space=pl.ANY)] * len(kept),
            out_specs=[placed, wide, thin, wide, thin, thin, thin, thin, side, side]
            + [pl.BlockSpec((sums, width), lambda at, index: (0, 0))],
            scratch_shapes=[
                pltpu.VMEM((units, devices, share, width), bf16),
                pltpu.VMEM((8, fold * width), f32),
                pltpu.VMEM((fold, tile, width), f32),
                pltpu.SemaphoreType.DMA((units,)),
            ],
        ),
        out_shape=[
            jax.ShapeDtypeStruct((seqs, rows, width), bf16),
            like(fold * width, bf16),
            like(width, bf16),
            like(fold * width, bf16),
            like(width, bf16),
            like(width, f32),
            like(width, bf16),
            like(width, bf16),
            like(width // 2, bf16),
            like(width // 2, bf16),
            jax.ShapeDtypeStruct((sums, width), f32),
        ],
        input_output_aliases={7: 0} if kept else {},
        compiler_params=pltpu.CompilerParams(vmem_limit_bytes=VMEM_LIMIT),
        cost_estimate=pl.CostEstimate(
            flops=4 * rows * width * width * (1 + 2 * fold),
            bytes_accessed=rows * width * (20 + 4 * fold) + 2 * units * width * width,
            transcendentals=rows * width * fold,
        ),
        name="feed",
    )(index, even, other, tokens, cotangent, gathered, second, *kept)


TN = ((0,), (0,))


def weight_grad_kernel(parts, *refs):
    groups = [refs[at * parts : (at + 1) * parts] for at in range(6)]
    active, grad_down, hidden, grad_up, context, attended = groups
    out_ref, block_ref, sems = refs[6 * parts :]
    devices, units, share, width = out_ref.shape
    fold = (units - 1) // 2
    group = devices // fold
    step = pl.program_id(0)
    slot = lax.rem(step, 2)

    def column_copy(unit, slot):
        return pltpu.make_async_copy(block_ref.at[slot], out_ref.at[:, unit], sems.at[slot])

    def row_copy(at, slot):
        return pltpu.make_async_copy(
            block_ref.at[slot].reshape(group, fold, share, width),
            out_ref.at[pl.ds(group * at, group), pl.ds(1 + fold, fold)],
            sems.at[slot],
        )

    def store(left, right, slot):
        total = None
        for one, other in zip(left, right):
            part = dot_f32(one[...], other[...], TN)
            total = part if total is None else total + part
        block_ref[slot] = total.astype(block_ref.dtype).reshape(devices, share, width)

    @pl.when(step >= 2)
    def _():
        column_copy(0, slot).wait()

    @pl.when(step == 0)
    def _():
        store(context, attended, 0)
        column_copy(0, 0).start()

    @pl.when((step >= 1) & (step <= fold))
    def _():
        store(hidden, grad_up, slot)
        column_copy(step, slot).start()

    @pl.when(step > fold)
    def _():
        store(active, grad_down, slot)
        row_copy(step - 1 - fold, slot).start()

    @pl.when(step == 2 * fold)
    def _():
        column_copy(0, 0).wait()
        column_copy(0, 1).wait()


def weight_grads(parts, devices):
    rows, width = parts[0][4].shape
    fold = parts[0][0].shape[1] // width
    share, units = width // devices, 1 + 2 * fold
    whole = pl.BlockSpec((rows, width), lambda at: (0, 0))
    active = pl.BlockSpec((rows, width), lambda at: (0, jnp.maximum(at - 1 - fold, 0)))
    up = pl.BlockSpec((rows, width), lambda at: (0, jnp.clip(at - 1, 0, fold - 1)))
    specs = [active, whole, whole, up, whole, whole]
    return pl.pallas_call(
        functools.partial(weight_grad_kernel, len(parts)),
        grid=(1 + 2 * fold,),
        in_specs=[spec for spec in specs for _ in parts],
        out_specs=pl.BlockSpec(memory_space=pl.ANY),
        scratch_shapes=[
            pltpu.VMEM((2, devices, share, width), jnp.bfloat16),
            pltpu.SemaphoreType.DMA((2,)),
        ],
        out_shape=jax.ShapeDtypeStruct((devices, units, share, width), jnp.bfloat16),
        compiler_params=pltpu.CompilerParams(vmem_limit_bytes=VMEM_LIMIT),
        cost_estimate=pl.CostEstimate(
            flops=2 * len(parts) * rows * width * width * (1 + 2 * fold),
            bytes_accessed=2 * (len(parts) * rows + width) * width * units,
            transcendentals=0,
        ),
        name="weight_grads",
    )(*[part[at] for at in range(6) for part in parts])


def own_grads_kernel(
    count, core_ref, query_ref, key_ref, value_ref, own_ref, other_ref, *refs
):
    out_ref, sum_ref, bias_ref = refs[-3:]
    devices, high, wide = out_ref.shape
    cols, share = wide // 3, high - 8
    step = pl.program_id(0)

    @pl.when(step == 0)
    def _():
        sum_ref[...] = jnp.zeros_like(sum_ref)
        bias_ref[...] = jnp.zeros_like(bias_ref)

    tokens = block_rows(core_ref, own_ref, other_ref)
    for at, grad_ref in enumerate((query_ref, key_ref, value_ref)):
        grad = grad_ref[...]
        here = slice(at * cols, (at + 1) * cols)
        sum_ref[:, here] += dot_f32(tokens, grad, TN)
        bias_ref[0:1, here] += jnp.sum(grad.astype(jnp.float32), axis=0, keepdims=True)

    @pl.when(step == pl.num_programs(0) - 1)
    def _():
        out_ref[:, :share, :] = sum_ref[...].astype(out_ref.dtype).reshape(devices, share, wide)
        total = refs[0][...]
        for ref in refs[1:-3]:
            total = total + ref[...]
        zero = jnp.zeros((1, cols), jnp.float32)
        bits = [total[at : at + 1, low : low + cols] for at in range(count) for low in (0, cols)]
        bits += [zero] * (21 - len(bits))
        lines = [jnp.concatenate(bits[at : at + 3], axis=1) for at in range(0, 21, 3)]
        lines = jnp.concatenate([bias_ref[0:1, :]] + lines, axis=0).astype(out_ref.dtype)
        out_ref[:, share:, :] = jnp.broadcast_to(lines[None], (devices, 8, wide))


def own_grads(core, grads, own, other, sums, count, devices, half):
    length, width = 2 * own.shape[0], own.shape[1]
    share, wide = width // devices, 3 * (width // 2)
    grad_spec = pl.BlockSpec((2 * half, wide // 3), lambda at, core: (at, 0))
    return pl.pallas_call(
        functools.partial(own_grads_kernel, count),
        grid_spec=pltpu.PrefetchScalarGridSpec(
            num_scalar_prefetch=1,
            grid=(length // (2 * half),),
            in_specs=[grad_spec] * 3
            + block_specs(half, width)
            + [pl.BlockSpec(item.shape, lambda at, core: (0, 0)) for item in sums],
            out_specs=pl.BlockSpec((devices, share + 8, wide), lambda at, core: (0, 0, 0)),
            scratch_shapes=[
                pltpu.VMEM((width, wide), jnp.float32),
                pltpu.VMEM((8, wide), jnp.float32),
            ],
        ),
        out_shape=jax.ShapeDtypeStruct((devices, share + 8, wide), jnp.bfloat16),
        compiler_params=pltpu.CompilerParams(vmem_limit_bytes=VMEM_LIMIT),
        cost_estimate=pl.CostEstimate(
            flops=2 * length * width * wide, bytes_accessed=6 * length * width, transcendentals=0
        ),
        name="own_grads",
    )(core, *grads, own, other, *sums)


def tokens_grad_kernel(
    share, core_ref, query_ref, key_ref, value_ref, gathered_ref, own_ref, other_ref
):
    total = None
    for at, grad_ref in enumerate((query_ref, key_ref, value_ref)):
        part = dot_f32(grad_ref[...], own_weight(gathered_ref, at, share), NT)
        total = part if total is None else total + part
    half = own_ref.shape[0]
    total = total.astype(own_ref.dtype)
    first = core_ref[0] == 0
    own_ref[...] = jnp.where(first, total[:half], total[half:])
    other_ref[...] = jnp.where(first, total[half:], total[:half])


def tokens_grads(core, grads, gathered, half):
    length, width = grads[0].shape[0], 2 * gathered.shape[4]
    cols, share = width // 2, (gathered.shape[3] - 8) // 3
    rows = jax.ShapeDtypeStruct((length // 2, width), jnp.bfloat16)
    return pl.pallas_call(
        functools.partial(tokens_grad_kernel, share),
        grid_spec=pltpu.PrefetchScalarGridSpec(
            num_scalar_prefetch=1,
            grid=(length // (2 * half),),
            in_specs=[pl.BlockSpec((2 * half, cols), lambda at, core: (at, 0))] * 3
            + [pl.BlockSpec(gathered.shape, lambda at, core: (0,) * 5)],
            out_specs=block_specs(half, width),
        ),
        out_shape=[rows, rows],
        compiler_params=pltpu.CompilerParams(vmem_limit_bytes=VMEM_LIMIT),
        cost_estimate=pl.CostEstimate(
            flops=6 * length * width * cols, bytes_accessed=6 * length * width, transcendentals=0
        ),
        name="tokens_grads",
    )(core, *grads, gathered)


def body(
    tokens,
    cotangent,
    lengths,
    query_weight,
    key_weight,
    value_weight,
    output_weight,
    up_weight,
    down_weight,
    query_bias,
    value_bias,
    output_bias,
    up_bias,
    down_bias,
    attn_gain,
    attn_shift,
    ffn_gain,
    ffn_shift,
):
    seqs, stretch, width = tokens.shape
    rows = seqs * stretch
    n_pair, n_core, n_blk = (lax.axis_size(axis) for axis in ALL)
    devices = n_pair * n_core * n_blk
    pair, core, blk = (lax.axis_index(axis) for axis in ALL)
    half, cols = stretch // 2, width // 2
    own_rows = n_blk * half
    share = query_weight.shape[0]
    fold = up_weight.shape[1] // width
    bf16, f32 = jnp.bfloat16, jnp.float32

    def table(step, back):
        moves = []
        for pair in range(n_pair):
            for src_core in range(n_core):
                for src in range(n_blk):
                    piece = src ^ step
                    sender = (pair * n_core + src_core) * n_blk + src
                    target = (pair * n_core + piece % 2) * n_blk + seqs * src_core + piece // 2
                    moves.append((target, sender) if back else (sender, target))
        return moves

    def move(array, step, back=False):
        return lax.ppermute(array, ALL, table(step, back))

    def after(array, *others):
        return lax.optimization_barrier((array, others))[0]

    def other_core(array):
        return lax.ppermute(array, "core", [(0, 1), (1, 0)])

    def columns(array, which):
        return lax.dynamic_slice_in_dim(array, which * cols, cols, axis=-1)

    def swap(flip, one, two):
        return jnp.where(flip, two, one), jnp.where(flip, one, two)

    def ordered(me, items):
        bit = 1
        while bit < len(items):
            flip = (me & bit) != 0
            items = [jnp.where(flip, items[at ^ bit], items[at]) for at in range(len(items))]
            bit *= 2
        return items

    def others(array, axis, size):
        return [
            lax.ppermute(array, axis, [(at, at ^ step) for at in range(size)])
            for step in range(1, size)
        ]

    which = jnp.reshape(core, (1,)).astype(jnp.int32)
    mine, theirs, second = pack(
        which,
        (query_weight, key_weight, value_weight, output_weight, up_weight, down_weight),
        (query_bias, value_bias, output_bias, up_bias, down_bias)
        + (attn_gain, attn_shift, ffn_gain, ffn_shift),
    )
    gathered = jnp.stack(swap(core == 1, mine, other_core(theirs)))
    gathered = jnp.stack(ordered(blk, [gathered] + others(gathered, "blk", n_blk)))
    tokens_moved = after(tokens, gathered)
    seconds = lax.all_gather(second, "blk", axis=0)
    pieces = tokens_moved.reshape(n_blk, half, width)
    arrived = [
        move(lax.dynamic_index_in_dim(pieces, blk ^ step, 0, keepdims=False), step)
        for step in range(n_blk)
    ]
    terms, arrived[:2] = lax.optimization_barrier(
        ([gathered] + others(gathered, "pair", n_pair), arrived[:2])
    )
    gathered = jnp.stack(ordered(pair, terms))
    second = lax.all_gather(after(seconds, gathered), ("pair", "core"), axis=0)
    second = second.reshape((devices,) + second.shape[2:])
    both = jnp.concatenate(swap(core == 1, lengths, other_core(lengths)))
    own_length = lax.dynamic_index_in_dim(both, blk, 0, keepdims=False)

    parts = n_blk // 2
    piece = 2 * (blk % seqs) + core
    info = jnp.stack(
        [own_length] + [(piece ^ (at // 2)) * stretch + at % 2 * half for at in range(2 * n_blk)]
    ).astype(jnp.int32)
    own_tokens = after(jnp.concatenate(arrived, axis=0), gathered, info)
    other_tokens = other_core(own_tokens)
    odd = blk % 2 == 1

    def after_all(items, *others):
        return lax.optimization_barrier((items, others))[0]

    qkv = project(which, own_tokens, other_tokens, gathered, half)
    attended, returning = [], []
    for part in range(parts):
        query_side = after(qkv, attended[-1]) if part else qkv
        attended.append(attend(query_side, info, part, parts, 512))
        returning.append([move(attended[-1][at], 2 * part + at, True) for at in range(2)])

    fed, context_grads, kept = [], [], ()
    for part in range(parts):
        even, other = after_all(returning[part], fed[-1] if part else attended[-1])
        index = jnp.stack([(blk // 2) ^ part, blk % 2]).astype(jnp.int32)
        fed.append(feed(index, even, other, tokens, cotangent, gathered, second, kept, 256))
        kept = (fed[-1][0],)
        context_grads.append([move(fed[-1][8 + at], 2 * part + at) for at in range(2)])
    layer_out = kept[0]

    early, late = context_grads[0], context_grads[1]
    early, first_active = lax.optimization_barrier((early, fed[0][1]))
    second_grads = weight_grads(
        [
            (item[1] if part else first_active, item[2], item[4], item[3], item[7], item[6])
            for part, item in enumerate(fed)
        ],
        devices,
    )
    late, second_grads = lax.optimization_barrier((late, second_grads))
    total = second_grads
    second_grads = lax.psum_scatter(
        second_grads.reshape((n_pair * n_core, n_blk) + second_grads.shape[1:]),
        ("pair", "core"),
        scatter_dimension=0,
    )
    early[0] = after(early[0], total)
    outs, auxes = [item[2] for item in attended], [item[3] for item in attended]
    grads = attend_back(qkv, list(early) + list(late), outs, auxes, info, 512, 1024)

    own, far = tokens_grads(which, grads, gathered, half)
    summed = (own.astype(f32) + other_core(far).astype(f32)).astype(bf16)
    moved = [move(summed[step * half : (step + 1) * half], step, True) for step in range(n_blk)]
    second_grads, summed = lax.optimization_barrier((second_grads, summed))
    second_grads = lax.psum_scatter(second_grads, "blk", scatter_dimension=0)
    first_grads = own_grads(
        which,
        [after(item, summed) for item in grads],
        own_tokens,
        other_tokens,
        [item[10] for item in fed],
        6 + fold,
        devices,
        half,
    )
    first_grads, moved[0] = lax.optimization_barrier((first_grads, moved[0]))

    def to_sum(array, axis, me, size):
        terms = [lax.dynamic_index_in_dim(array, me, 0, keepdims=False)]
        for step in range(1, size):
            sent = lax.dynamic_index_in_dim(array, me ^ step, 0, keepdims=False)
            terms.append(lax.ppermute(sent, axis, [(at, at ^ step) for at in range(size)]))
        return terms

    def add(terms):
        total = terms[0].astype(f32)
        for term in terms[1:]:
            total += term.astype(f32)
        return total.astype(bf16)

    first_grads = first_grads.reshape(n_pair, n_core, n_blk, share + 8, 3 * cols)
    total = add(to_sum(first_grads, "pair", pair, n_pair))
    moved[1:], total = lax.optimization_barrier((moved[1:], total))
    terms = to_sum(jnp.moveaxis(total, 1, 0), "blk", blk, n_blk)
    returned = []
    for part in range(parts):
        back = jnp.concatenate(swap(odd, *moved[2 * part : 2 * part + 2]), axis=0)
        returned.append(fed[part][5] + back.astype(f32))
    tokens_grad = jnp.stack(swap(blk >= 2, *returned))

    device = (pair * n_core + core) * n_blk + blk

    def own_part(line, size):
        return lax.dynamic_slice_in_dim(line, device * size, size, axis=-1)

    second_grads = second_grads.astype(f32)
    late = (
        second_grads[0],
        jnp.concatenate([second_grads[1 + at] for at in range(fold)], axis=1),
        second_grads[1 + fold :].reshape(fold * share, width),
    )
    terms, tokens_grad, late = lax.optimization_barrier((terms, tokens_grad, late))
    total = add(terms)
    kept = lax.dynamic_index_in_dim(total, core, 0, keepdims=False)
    crossed = other_core(lax.dynamic_index_in_dim(total, 1 - core, 0, keepdims=False))
    left, right = (item.astype(f32) for item in swap(core == 1, kept, crossed))
    projections = [
        jnp.concatenate([left[:, at : at + cols], right[:, at : at + cols]], axis=1)
        for at in range(0, 3 * cols, cols)
    ]
    lines = (kept[share + 1 :].astype(f32) + crossed[share + 1 :].astype(f32)).reshape(-1)
    own_lines = own_part(lines[: 6 * width].reshape(6, width), share)
    up_line = own_part(lines[6 * width : (6 + fold) * width], fold * share)
    return (
        (layer_out, tokens_grad)
        + tuple(item[:share] for item in projections)
        + late
        + (own_part(projections[0][share], share), own_part(projections[2][share], share))
        + (own_lines[0], up_line, own_lines[1], own_lines[2], own_lines[3], own_lines[4], own_lines[5])
    )


def fits(mesh, tokens, up_weight):
    n_dp, n_blk = mesh.shape["dp"], mesh.shape["blk"]
    batch, length, width = tokens.shape
    if n_dp % 2 or n_dp & (n_dp - 1) or batch % n_dp or 2 * (batch // n_dp) != n_blk or n_blk != 4:
        return False
    share = width // (n_dp * n_blk)
    fold = up_weight.shape[1] // width
    return (
        width == HEADS * 64
        and width % (4 * LANES // PER_TILE) == 0
        and up_weight.shape[1] == fold * width
        and share * n_dp * n_blk == width
        and share % 8 == 0
        and 16 <= share
        and (8 + fold) * share <= width // 2
        and fold == 4
        and length % (16 * n_blk) == 0
        and length % 512 == 0
        and length <= 4096
    )


def solution(mesh):
    n_dp, n_blk = mesh.shape["dp"], mesh.shape["blk"]

    def step(*args):
        spread = ("dp", "blk")
        one, use = ring_body, mesh
        where = {"dp": "dp", "blk": "blk", spread: spread}
        if fits(mesh, args[0], args[7]):
            one, use = body, Mesh(mesh.devices.reshape(n_dp // 2, 2, n_blk), ALL)
            where = {"dp": ("pair", "core"), "blk": "blk", spread: ALL}
        block = P(where["dp"], where["blk"], None)
        matrix = P(where[spread], None)
        vector = P(where[spread])
        return jax.shard_map(
            one,
            mesh=use,
            in_specs=(block, block, P(where["dp"])) + (matrix,) * 6 + (vector,) * 9,
            out_specs=(block, block) + (matrix,) * 6 + (vector,) * 9,
            check_vma=False,
        )(*args)

    return step
```

profile of v0, /device:TPU:9, one launch (start us, length us, event | category | flops | bytes accessed | tf_op | source)
XLA Modules:
  0.0 408.8 jit_solution(8780720008394027490)
XLA Ops:
  7.3 2.2 pack.1
  15.8 7.3 %collective-permute-done.2 = bf16[2,80,384]{2,1,0:T(8,128)(2,1)S(1)} collective-permute-done((bf16[2,80,384]{2,1,0:T(8,128)(2,1)S(1)}, bf16[2,80,384]{2,1,0:T(8,128)(2,1)S(1)}, u32[]{:S(2)}, u32[]{:S(2)}) %collective-permute-start.2) | collective-permute-done | bytes 122912 | tf_op jit(solution)/shard_map/ppermute | solution.py:1111
  23.1 5.3 %collective-permute-done.3 = bf16[2,80,384]{2,1,0:T(8,128)(2,1)S(1)} collective-permute-done((bf16[2,80,384]{2,1,0:T(8,128)(2,1)S(1)}, bf16[2,80,384]{2,1,0:T(8,128)(2,1)S(1)}, u32[]{:S(2)}, u32[]{:S(2)}) %collective-permute-start.3) | collective-permute-done | bytes 122912 | tf_op jit(solution)/shard_map/ppermute | solution.py:1111
  32.4 3.9 collective-permute-start.8
  36.3 6.3 %collective-permute-start.9 = (bf16[256,768]{1,0:T(8,128)(2,1)}, bf16[256,768]{1,0:T(8,128)(2,1)S(1)}, u32[]{:S(2)}, u32[]{:S(2)}) collective-permute-start(bf16[256,768]{1,0:T(8,128)(2,1)} %get-tuple-element.186), channel_id=1, source_target_pairs={{0,4},{1,0},{2,5},{3,1},{4,6},{5,2},{6,7},{7,3},{8,12},{9,8},{10,1... | collective-permute-start | bytes 1179656 | tf_op jit(solution)/shard_map/ppermute | solution.py:1087
  42.6 16.1 %collective-permute-done.8 = bf16[256,768]{1,0:T(8,128)(2,1)S(1)} collective-permute-done((bf16[256,768]{1,0:T(8,128)(2,1)}, bf16[256,768]{1,0:T(8,128)(2,1)S(1)}, u32[]{:S(2)}, u32[]{:S(2)}) %collective-permute-start.8) | collective-permute-done | bytes 393248 | tf_op jit(solution)/shard_map/ppermute | solution.py:1087
  58.7 4.7 %collective-permute-done.9 = bf16[256,768]{1,0:T(8,128)(2,1)S(1)} collective-permute-done((bf16[256,768]{1,0:T(8,128)(2,1)}, bf16[256,768]{1,0:T(8,128)(2,1)S(1)}, u32[]{:S(2)}, u32[]{:S(2)}) %collective-permute-start.9) | collective-permute-done | bytes 393248 | tf_op jit(solution)/shard_map/ppermute | solution.py:1087
  67.9 3.1 collective-permute-start.10
  74.1 3.1 collective-permute-done.11
  77.1 3.5 collective-permute-done.10
  82.8 2.6 collective-permute-done.12.other_ref
  85.4 8.9 %project.1.query_ref.key_ref.value_ref = bf16[2048,1152]{1,0:T(8,128)(2,1)} custom-call(s32[1]{0:T(128)} %bitcast.10.core_ref, bf16[1024,768]{1,0:T(8,128)(2,1)} %copy-done, bf16[1024,768]{1,0:T(8,128)(2,1)} %collective-permute-done.12.other_ref, bf16[4,4,2,80,384]{4,3,2,1,0:T(8,128)(2,1)} %pad_maximum_fusion.1.gathered_ref.small_ref), custom_call_target="tpu_custom_call" | custom-call | flops 3623878656 | bytes 15728640 | tf_op jit(solution)/shard_map/project/pallas_call | solution.py:652
  94.3 19.4 %attend.2 = (bf16[512,384]{1,0:T(8,128)(2,1)}, bf16[512,384]{1,0:T(8,128)(2,1)}, f32[1024,384]{1,0:T(8,128)}, bf16[1024,384]{1,0:T(8,128)(2,1)}) custom-call(s32[9]{0:T(128)} %stack.103.info_ref, bf16[2048,1152]{1,0:T(8,128)(2,1)} %project.1.query_ref.key_ref.value_ref, bf16[2048,1152]{1,0:T(8,128)(2,1)} %project.1.query_ref.key_ref.value_ref, ...), custom_call_target="tpu_custom_call" | custom-call | flops 12884901888 | bytes 9437184 | tf_op jit(solution)/shard_map/attend/pallas_call | solution.py:382
  113.7 3.7 collective-permute-start.15
  117.4 3.7 collective-permute-start.16
  121.1 19.5 %attend.3 = (bf16[512,384]{1,0:T(8,128)(2,1)}, bf16[512,384]{1,0:T(8,128)(2,1)}, f32[1024,384]{1,0:T(8,128)}, bf16[1024,384]{1,0:T(8,128)(2,1)}) custom-call(s32[9]{0:T(128)} %stack.103.info_ref, bf16[2048,1152]{1,0:T(8,128)(2,1)} %project.1.query_ref.key_ref.value_ref, bf16[2048,1152]{1,0:T(8,128)(2,1)} %project.1.query_ref.key_ref.value_ref, ...), custom_call_target="tpu_custom_call" | custom-call | flops 12884901888 | bytes 9437184 | tf_op jit(solution)/shard_map/attend/pallas_call | solution.py:382
  140.6 3.5 collective-permute-start.14
  145.0 24.7 %feed.2 = (bf16[2,512,768]{2,1,0:T(8,128)(2,1)}, bf16[512,3072]{1,0:T(8,128)(2,1)}, bf16[512,768]{1,0:T(8,128)(2,1)}, bf16[512,3072]{1,0:T(8,128)(2,1)}, bf16[51...) custom-call(s32[2]{0:T(128)} %get-tuple-element.226.index_ref, ...), custom_call_target="tpu_custom_call" | custom-call | flops 10871635968 | bytes 24772608 | tf_op jit(solution)/shard_map/feed/pallas_call | solution.py:814
  174.7 24.7 %feed.3 = (bf16[2,512,768]{2,1,0:T(8,128)(2,1)}, bf16[512,3072]{1,0:T(8,128)(2,1)}, bf16[512,768]{1,0:T(8,128)(2,1)}, bf16[512,3072]{1,0:T(8,128)(2,1)}, bf16[51...) custom-call(s32[2]{0:T(128)} %get-tuple-element.225.index_ref, ...), custom_call_target="tpu_custom_call", output_to_operand_aliasing={{0}: (7, {})} | custom-call | flops 10871635968 | bytes 24772608 | tf_op jit(solution)/shard_map/feed/pallas_call | solution.py:814
  200.6 4.5 %collective-permute-start.20 = (bf16[512,384]{1,0:T(8,128)(2,1)}, bf16[512,384]{1,0:T(8,128)(2,1)S(1)}, u32[]{:S(2)}, u32[]{:S(2)}) collective-permute-start(bf16[512,384]{1,0:T(8,128)(2,1)} %get-tuple-element.134), channel_id=1, source_target_pairs={{0,5},{1,1},{2,4},{3,0},{4,7},{5,3},{6,6},{7,2},{8,13},{9,9},{10,1... | collective-permute-start | bytes 1179656 | tf_op jit(solution)/shard_map/ppermute | solution.py:1087
  205.1 19.5 %weight_grads.1 = bf16[32,9,24,768]{3,2,1,0:T(8,128)(2,1)} custom-call(bf16[512,3072]{1,0:T(8,128)(2,1)} %get-tuple-element.135.refs_0_, bf16[512,3072]{1,0:T(8,128)(2,1)} %get-tuple-element.136.refs_1_, bf16[512,768]{1,0:T(8,128)(2,1)} %get-tuple-element.120.refs_2_, bf16[512,768]{1,0:T(8,128)(2,1)} %get-tuple-element.137.refs_3_, ...), custom_call_target="tpu_custom_call" | custom-call | flops 10871635968 | bytes 24772608 | tf_op jit(solution)/shard_map/weight_grads/pallas_call | solution.py:927
  225.5 73.2 %attend_back.1 = (bf16[2048,384]{1,0:T(8,128)(2,1)}, bf16[2048,384]{1,0:T(8,128)(2,1)}, bf16[2048,384]{1,0:T(8,128)(2,1)}) custom-call(s32[9]{0:T(128)} %stack.103.info_ref, bf16[2048,1152]{1,0:T(8,128)(2,1)} %project.1.query_ref.key_ref.value_ref, bf16[2048,1152]{1,0:T(8,128)(2,1)} %project.1.query_ref.key_ref.value_ref, ...), custom_call_target="tpu_custom_call" | custom-call | flops 64424509440 | bytes 17301504 | tf_op jit(solution)/shard_map/attend_back/pallas_call | solution.py:487
  298.7 8.8 %tokens_grads.1 = (bf16[1024,768]{1,0:T(8,128)(2,1)}, bf16[1024,768]{1,0:T(8,128)(2,1)}) custom-call(s32[1]{0:T(128)} %bitcast.10.core_ref, bf16[2048,384]{1,0:T(8,128)(2,1)} %get-tuple-element.153.query_ref, bf16[2048,384]{1,0:T(8,128)(2,1)} %get-tuple-element.154.key_ref, bf16[2048,384]{1,0:T(8,128)(2,1)} %get-tuple-element.155.value_ref, ...), custom_call_target="tpu_custom_call" | custom-call | flops 3623878656 | bytes 9437184 | tf_op jit(solution)/shard_map/tokens_grads/pallas_call | solution.py:1026
  307.5 3.6 collective-permute-done.21
  314.0 2.8 collective-permute-start.25
  316.9 9.4 %own_grads.1 = bf16[32,32,1152]{2,1,0:T(8,128)(2,1)} custom-call(s32[1]{0:T(128)} %bitcast.10.core_ref, bf16[2048,384]{1,0:T(8,128)(2,1)} %get-tuple-element.153.query_ref, bf16[2048,384]{1,0:T(8,128)(2,1)} %get-tuple-element.154.key_ref, bf16[2048,384]{1,0:T(8,128)(2,1)} %get-tuple-element.155.value_ref, bf16[1024,768]{1,0:T(8,128)(2,1)} %copy-done, ...), custom_call_target="tpu_custom_call" | custom-call | flops 3623878656 | bytes 9437184 | tf_op jit(solution)/shard_map/own_grads/pallas_call | solution.py:985
  331.3 2.6 collective-permute-start.22
  335.0 9.6 %collective-permute-done.28 = bf16[2,4,32,1152]{3,2,1,0:T(8,128)(2,1)S(1)} collective-permute-done((bf16[2,4,32,1152]{3,2,1,0:T(8,128)(2,1)S(1)}, bf16[2,4,32,1152]{3,2,1,0:T(8,128)(2,1)S(1)}, u32[]{:S(2)}, u32[]{:S(2)}) %collective-permute-start.28) | collective-permute-done | bytes 589856 | tf_op jit(solution)/shard_map/ppermute | solution.py:1209
  346.6 10.6 %collective-permute-done.27 = bf16[2,4,32,1152]{3,2,1,0:T(8,128)(2,1)S(1)} collective-permute-done((bf16[2,4,32,1152]{3,2,1,0:T(8,128)(2,1)S(1)}, bf16[2,4,32,1152]{3,2,1,0:T(8,128)(2,1)S(1)}, u32[]{:S(2)}, u32[]{:S(2)}) %collective-permute-start.27) | collective-permute-done | bytes 589856 | tf_op jit(solution)/shard_map/ppermute | solution.py:1209
  358.6 20.9 %collective-permute-done.22 = bf16[256,768]{1,0:T(8,128)(2,1)S(1)} collective-permute-done((bf16[256,768]{1,0:T(8,128)(2,1)}, bf16[256,768]{1,0:T(8,128)(2,1)S(1)}, u32[]{:S(2)}, u32[]{:S(2)}) %collective-permute-start.22) | collective-permute-done | bytes 393248 | tf_op jit(solution)/shard_map/ppermute | solution.py:1087
  379.9 2.4 collective-permute-start.31
  387.9 7.9 %collective-permute-done.31 = bf16[2,32,1152]{2,1,0:T(8,128)(2,1)S(1)} collective-permute-done((bf16[2,32,1152]{2,1,0:T(8,128)(2,1)S(1)}, bf16[2,32,1152]{2,1,0:T(8,128)(2,1)S(1)}, u32[]{:S(2)}, u32[]{:S(2)}) %collective-permute-start.31) | collective-permute-done | bytes 147488 | tf_op jit(solution)/shard_map/ppermute | solution.py:1209
  (144 shorter events, 52.6 us)
Async XLA Ops:
  7.2 58.6 %all-gather.5.cloned.1.call-start = ((), (), s32[]{:S(2)}) async-start(), calls=%async_computation.4 | async-start | bytes 1658880 | tf_op jit(solution)/shard_map/all_gather | solution.py:1125
  9.5 134.7 %all-gather.7.cloned.1.call-start = ((), (), s32[]{:S(2)}) async-start(), calls=%async_computation.5 | async-start | bytes 11943936 | tf_op jit(solution)/shard_map/all_gather | solution.py:1135
  12.2 10.8 %collective-permute-start.2 = (bf16[2,80,384]{2,1,0:T(8,128)(2,1)S(1)}, bf16[2,80,384]{2,1,0:T(8,128)(2,1)S(1)}, u32[]{:S(2)}, u32[]{:S(2)}) collective-permute-start(bf16[2,80,384]{2,1,0:T(8,128)(2,1)S(1)} %pad_maximum_fusion.7), channel_id=1, source_target_pairs={{0,3},{1,2},{2,1},{3,0},{4,7},{5,6},{6,5},{7,4},{8,11},{9,10},{10,... | collective-permute-start | bytes 368648 | tf_op jit(solution)/shard_map/ppermute | solution.py:1111
  13.6 14.8 %collective-permute-start.3 = (bf16[2,80,384]{2,1,0:T(8,128)(2,1)S(1)}, bf16[2,80,384]{2,1,0:T(8,128)(2,1)S(1)}, u32[]{:S(2)}, u32[]{:S(2)}) collective-permute-start(bf16[2,80,384]{2,1,0:T(8,128)(2,1)S(1)} %pad_maximum_fusion.7), channel_id=1, source_target_pairs={{0,2},{1,3},{2,0},{3,1},{4,6},{5,7},{6,4},{7,5},{8,10},{9,11},{10,... | collective-permute-start | bytes 368648 | tf_op jit(solution)/shard_map/ppermute | solution.py:1111
  14.7 13.7 %collective-permute-start.4 = (bf16[2,80,384]{2,1,0:T(8,128)(2,1)S(1)}, bf16[2,80,384]{2,1,0:T(8,128)(2,1)S(1)}, u32[]{:S(2)}, u32[]{:S(2)}) collective-permute-start(bf16[2,80,384]{2,1,0:T(8,128)(2,1)S(1)} %pad_maximum_fusion.7), channel_id=1, source_target_pairs={{0,1},{1,0},{2,3},{3,2},{4,5},{5,4},{6,7},{7,6},{8,9},{9,8},{10,11... | collective-permute-start | bytes 368648 | tf_op jit(solution)/shard_map/ppermute | solution.py:1111
  28.6 34.9 %collective-permute-start.5 = (bf16[4,2,80,384]{3,2,1,0:T(8,128)(2,1)S(1)}, bf16[4,2,80,384]{3,2,1,0:T(8,128)(2,1)S(1)}, u32[]{:S(2)}, u32[]{:S(2)}) collective-permute-start(bf16[4,2,80,384]{3,2,1,0:T(8,128)(2,1)S(1)} %pad_maximum_fusion.5), channel_id=1, source_target_pairs={{0,8},{8,0},{16,24},{24,16},{1,9},{9,1},{17,25},{25,17},{2,10},{10... | collective-permute-start | bytes 1474568 | tf_op jit(solution)/shard_map/ppermute | solution.py:1111
  29.8 33.6 %collective-permute-start.6 = (bf16[4,2,80,384]{3,2,1,0:T(8,128)(2,1)S(1)}, bf16[4,2,80,384]{3,2,1,0:T(8,128)(2,1)S(1)}, u32[]{:S(2)}, u32[]{:S(2)}) collective-permute-start(bf16[4,2,80,384]{3,2,1,0:T(8,128)(2,1)S(1)} %pad_maximum_fusion.5), channel_id=1, source_target_pairs={{0,16},{8,24},{16,0},{24,8},{1,17},{9,25},{17,1},{25,9},{2,18},{10... | collective-permute-start | bytes 1474568 | tf_op jit(solution)/shard_map/ppermute | solution.py:1111
  31.1 32.4 %collective-permute-start.7 = (bf16[4,2,80,384]{3,2,1,0:T(8,128)(2,1)S(1)}, bf16[4,2,80,384]{3,2,1,0:T(8,128)(2,1)S(1)}, u32[]{:S(2)}, u32[]{:S(2)}) collective-permute-start(bf16[4,2,80,384]{3,2,1,0:T(8,128)(2,1)S(1)} %pad_maximum_fusion.5), channel_id=1, source_target_pairs={{0,24},{8,16},{16,8},{24,0},{1,25},{9,17},{17,9},{25,1},{2,26},{10... | collective-permute-start | bytes 1474568 | tf_op jit(solution)/shard_map/ppermute | solution.py:1111
  32.4 26.3 %collective-permute-start.8 = (bf16[256,768]{1,0:T(8,128)(2,1)}, bf16[256,768]{1,0:T(8,128)(2,1)S(1)}, u32[]{:S(2)}, u32[]{:S(2)}) collective-permute-start(bf16[256,768]{1,0:T(8,128)(2,1)} %get-tuple-element.189), channel_id=1, source_target_pairs={{0,0},{1,4},{2,1},{3,5},{4,2},{5,6},{6,3},{7,7},{8,8},{9,12},{10,9... | collective-permute-start | bytes 1179656 | tf_op jit(solution)/shard_map/ppermute | solution.py:1087
  36.3 27.1 %collective-permute-start.9 = (bf16[256,768]{1,0:T(8,128)(2,1)}, bf16[256,768]{1,0:T(8,128)(2,1)S(1)}, u32[]{:S(2)}, u32[]{:S(2)}) collective-permute-start(bf16[256,768]{1,0:T(8,128)(2,1)} %get-tuple-element.186), channel_id=1, source_target_pairs={{0,4},{1,0},{2,5},{3,1},{4,6},{5,2},{6,7},{7,3},{8,12},{9,8},{10,1... | collective-permute-start | bytes 1179656 | tf_op jit(solution)/shard_map/ppermute | solution.py:1087
  65.8 251.1 %reduce-scatter.3.cloned.1.call-start = ((), (), s32[]{:S(2)}) async-start(), calls=%async_computation.2 | async-start | bytes 11943936 | tf_op jit(solution)/shard_map/reduce_scatter | solution.py:1179
  65.8 11.3 %collective-permute-start.11 = (bf16[256,768]{1,0:T(8,128)(2,1)S(1)}, bf16[256,768]{1,0:T(8,128)(2,1)S(1)}, u32[]{:S(2)}, u32[]{:S(2)}) collective-permute-start(bf16[256,768]{1,0:T(8,128)(2,1)S(1)} %copy-done.12), channel_id=1, source_target_pairs={{0,5},{1,1},{2,4},{3,0},{4,7},{5,3},{6,6},{7,2},{8,13},{9,9},{10,1... | collective-permute-start | bytes 1179656 | tf_op jit(solution)/shard_map/ppermute | solution.py:1087
  67.9 12.7 %collective-permute-start.10 = (bf16[256,768]{1,0:T(8,128)(2,1)S(1)}, bf16[256,768]{1,0:T(8,128)(2,1)S(1)}, u32[]{:S(2)}, u32[]{:S(2)}) collective-permute-start(bf16[256,768]{1,0:T(8,128)(2,1)S(1)} %copy-done.11), channel_id=1, source_target_pairs={{0,1},{1,5},{2,0},{3,4},{4,3},{5,7},{6,2},{7,6},{8,9},{9,13},{10,8... | collective-permute-start | bytes 1179656 | tf_op jit(solution)/shard_map/ppermute | solution.py:1087
  113.7 30.4 %collective-permute-start.15 = (bf16[512,384]{1,0:T(8,128)(2,1)}, bf16[512,384]{1,0:T(8,128)(2,1)S(1)}, u32[]{:S(2)}, u32[]{:S(2)}) collective-permute-start(bf16[512,384]{1,0:T(8,128)(2,1)} %get-tuple-element.105), channel_id=1, source_target_pairs={{0,0},{4,1},{1,2},{5,3},{2,4},{6,5},{3,6},{7,7},{8,8},{12,9},{9,10... | collective-permute-start | bytes 1179656 | tf_op jit(solution)/shard_map/ppermute | solution.py:1087
  117.4 26.7 %collective-permute-start.16 = (bf16[512,384]{1,0:T(8,128)(2,1)}, bf16[512,384]{1,0:T(8,128)(2,1)S(1)}, u32[]{:S(2)}, u32[]{:S(2)}) collective-permute-start(bf16[512,384]{1,0:T(8,128)(2,1)} %get-tuple-element.106), channel_id=1, source_target_pairs={{4,0},{0,1},{5,2},{1,3},{6,4},{2,5},{7,6},{3,7},{12,8},{8,9},{13,1... | collective-permute-start | bytes 1179656 | tf_op jit(solution)/shard_map/ppermute | solution.py:1087
  140.6 33.1 %collective-permute-start.13 = (bf16[512,384]{1,0:T(8,128)(2,1)}, bf16[512,384]{1,0:T(8,128)(2,1)S(1)}, u32[]{:S(2)}, u32[]{:S(2)}) collective-permute-start(bf16[512,384]{1,0:T(8,128)(2,1)} %get-tuple-element.110), channel_id=1, source_target_pairs={{1,0},{5,1},{0,2},{4,3},{3,4},{7,5},{2,6},{6,7},{9,8},{13,9},{8,10... | collective-permute-start | bytes 1179656 | tf_op jit(solution)/shard_map/ppermute | solution.py:1087
  140.6 33.1 %collective-permute-start.14 = (bf16[512,384]{1,0:T(8,128)(2,1)}, bf16[512,384]{1,0:T(8,128)(2,1)S(1)}, u32[]{:S(2)}, u32[]{:S(2)}) collective-permute-start(bf16[512,384]{1,0:T(8,128)(2,1)} %get-tuple-element.111), channel_id=1, source_target_pairs={{5,0},{1,1},{4,2},{0,3},{7,4},{3,5},{6,6},{2,7},{13,8},{9,9},{12,1... | collective-permute-start | bytes 1179656 | tf_op jit(solution)/shard_map/ppermute | solution.py:1087
  169.7 35.3 %collective-permute-start.17 = (bf16[512,384]{1,0:T(8,128)(2,1)}, bf16[512,384]{1,0:T(8,128)(2,1)S(1)}, u32[]{:S(2)}, u32[]{:S(2)}) collective-permute-start(bf16[512,384]{1,0:T(8,128)(2,1)} %get-tuple-element.126), channel_id=1, source_target_pairs={{0,0},{1,4},{2,1},{3,5},{4,2},{5,6},{6,3},{7,7},{8,8},{9,12},{10,9... | collective-permute-start | bytes 1179656 | tf_op jit(solution)/shard_map/ppermute | solution.py:1087
  171.6 33.4 %collective-permute-start.18 = (bf16[512,384]{1,0:T(8,128)(2,1)}, bf16[512,384]{1,0:T(8,128)(2,1)S(1)}, u32[]{:S(2)}, u32[]{:S(2)}) collective-permute-start(bf16[512,384]{1,0:T(8,128)(2,1)} %get-tuple-element.127), channel_id=1, source_target_pairs={{0,4},{1,0},{2,5},{3,1},{4,6},{5,2},{6,7},{7,3},{8,12},{9,8},{10,1... | collective-permute-start | bytes 1179656 | tf_op jit(solution)/shard_map/ppermute | solution.py:1087
  199.4 25.2 %collective-permute-start.19 = (bf16[512,384]{1,0:T(8,128)(2,1)}, bf16[512,384]{1,0:T(8,128)(2,1)S(1)}, u32[]{:S(2)}, u32[]{:S(2)}) collective-permute-start(bf16[512,384]{1,0:T(8,128)(2,1)} %get-tuple-element.133), channel_id=1, source_target_pairs={{0,1},{1,5},{2,0},{3,4},{4,3},{5,7},{6,2},{7,6},{8,9},{9,13},{10,8... | collective-permute-start | bytes 1179656 | tf_op jit(solution)/shard_map/ppermute | solution.py:1087
  200.6 24.0 %collective-permute-start.20 = (bf16[512,384]{1,0:T(8,128)(2,1)}, bf16[512,384]{1,0:T(8,128)(2,1)S(1)}, u32[]{:S(2)}, u32[]{:S(2)}) collective-permute-start(bf16[512,384]{1,0:T(8,128)(2,1)} %get-tuple-element.134), channel_id=1, source_target_pairs={{0,5},{1,1},{2,4},{3,0},{4,7},{5,3},{6,6},{7,2},{8,13},{9,9},{10,1... | collective-permute-start | bytes 1179656 | tf_op jit(solution)/shard_map/ppermute | solution.py:1087
  225.5 159.2 %reduce-scatter.5.cloned.1.call-start = ((), (), s32[]{:S(2)}) async-start(), calls=%async_computation.3 | async-start | bytes 1658880 | tf_op jit(solution)/shard_map/reduce_scatter | solution.py:1192
  314.0 12.2 %collective-permute-start.25 = (bf16[256,768]{1,0:T(8,128)(2,1)S(1)}, bf16[256,768]{1,0:T(8,128)(2,1)S(1)}, u32[]{:S(2)}, u32[]{:S(2)}) collective-permute-start(bf16[256,768]{1,0:T(8,128)(2,1)S(1)} %get-tuple-element.182), channel_id=1, source_target_pairs={{0,0},{4,1},{1,2},{5,3},{2,4},{6,5},{3,6},{7,7},{8,8},{12,9},{9,10... | collective-permute-start | bytes 1179656 | tf_op jit(solution)/shard_map/ppermute | solution.py:1087
  328.6 16.0 %collective-permute-start.28 = (bf16[2,4,32,1152]{3,2,1,0:T(8,128)(2,1)S(1)}, bf16[2,4,32,1152]{3,2,1,0:T(8,128)(2,1)S(1)}, u32[]{:S(2)}, u32[]{:S(2)}) collective-permute-start(bf16[2,4,32,1152]{3,2,1,0:T(8,128)(2,1)S(1)} %get-tuple-element.176), channel_id=1, source_target_pairs={{0,24},{8,16},{16,8},{24,0},{1,25},{9,17},{17,9},{25,1},{2,26},{10... | collective-permute-start | bytes 1769480 | tf_op jit(solution)/shard_map/ppermute | solution.py:1209
  329.4 27.8 %collective-permute-start.27 = (bf16[2,4,32,1152]{3,2,1,0:T(8,128)(2,1)S(1)}, bf16[2,4,32,1152]{3,2,1,0:T(8,128)(2,1)S(1)}, u32[]{:S(2)}, u32[]{:S(2)}) collective-permute-start(bf16[2,4,32,1152]{3,2,1,0:T(8,128)(2,1)S(1)} %get-tuple-element.177), channel_id=1, source_target_pairs={{0,16},{8,24},{16,0},{24,8},{1,17},{9,25},{17,1},{25,9},{2,18},{10... | collective-permute-start | bytes 1769480 | tf_op jit(solution)/shard_map/ppermute | solution.py:1209
  330.8 26.4 %collective-permute-start.26 = (bf16[2,4,32,1152]{3,2,1,0:T(8,128)(2,1)S(1)}, bf16[2,4,32,1152]{3,2,1,0:T(8,128)(2,1)S(1)}, u32[]{:S(2)}, u32[]{:S(2)}) collective-permute-start(bf16[2,4,32,1152]{3,2,1,0:T(8,128)(2,1)S(1)} %get-tuple-element.175), channel_id=1, source_target_pairs={{0,8},{8,0},{16,24},{24,16},{1,9},{9,1},{17,25},{25,17},{2,10},{10... | collective-permute-start | bytes 1769480 | tf_op jit(solution)/shard_map/ppermute | solution.py:1209
  331.3 48.1 %collective-permute-start.22 = (bf16[256,768]{1,0:T(8,128)(2,1)}, bf16[256,768]{1,0:T(8,128)(2,1)S(1)}, u32[]{:S(2)}, u32[]{:S(2)}) collective-permute-start(bf16[256,768]{1,0:T(8,128)(2,1)} %get-tuple-element.185), channel_id=1, source_target_pairs={{4,0},{0,1},{5,2},{1,3},{6,4},{2,5},{7,6},{3,7},{12,8},{8,9},{13,1... | collective-permute-start | bytes 1179656 | tf_op jit(solution)/shard_map/ppermute | solution.py:1087
  333.9 45.6 %collective-permute-start.23 = (bf16[256,768]{1,0:T(8,128)(2,1)}, bf16[256,768]{1,0:T(8,128)(2,1)S(1)}, u32[]{:S(2)}, u32[]{:S(2)}) collective-permute-start(bf16[256,768]{1,0:T(8,128)(2,1)} %get-tuple-element.184), channel_id=1, source_target_pairs={{1,0},{5,1},{0,2},{4,3},{3,4},{7,5},{2,6},{6,7},{9,8},{13,9},{8,10... | collective-permute-start | bytes 1179656 | tf_op jit(solution)/shard_map/ppermute | solution.py:1087
  344.6 34.9 %collective-permute-start.24 = (bf16[256,768]{1,0:T(8,128)(2,1)}, bf16[256,768]{1,0:T(8,128)(2,1)S(1)}, u32[]{:S(2)}, u32[]{:S(2)}) collective-permute-start(bf16[256,768]{1,0:T(8,128)(2,1)} %get-tuple-element.183), channel_id=1, source_target_pairs={{5,0},{1,1},{4,2},{0,3},{7,4},{3,5},{6,6},{2,7},{13,8},{9,9},{12,1... | collective-permute-start | bytes 1179656 | tf_op jit(solution)/shard_map/ppermute | solution.py:1087
  379.5 8.3 %collective-permute-start.29 = (bf16[2,32,1152]{2,1,0:T(8,128)(2,1)S(1)}, bf16[2,32,1152]{2,1,0:T(8,128)(2,1)S(1)}, u32[]{:S(2)}, u32[]{:S(2)}) collective-permute-start(bf16[2,32,1152]{2,1,0:T(8,128)(2,1)S(1)} %get-tuple-element.201), channel_id=1, source_target_pairs={{0,1},{1,0},{2,3},{3,2},{4,5},{5,4},{6,7},{7,6},{8,9},{9,8},{10,11... | collective-permute-start | bytes 442376 | tf_op jit(solution)/shard_map/ppermute | solution.py:1209
  379.9 8.0 %collective-permute-start.30 = (bf16[2,32,1152]{2,1,0:T(8,128)(2,1)S(1)}, bf16[2,32,1152]{2,1,0:T(8,128)(2,1)S(1)}, u32[]{:S(2)}, u32[]{:S(2)}) collective-permute-start(bf16[2,32,1152]{2,1,0:T(8,128)(2,1)S(1)} %get-tuple-element.200), channel_id=1, source_target_pairs={{0,2},{1,3},{2,0},{3,1},{4,6},{5,7},{6,4},{7,5},{8,10},{9,11},{10,... | collective-permute-start | bytes 442376 | tf_op jit(solution)/shard_map/ppermute | solution.py:1209
  379.9 16.0 %collective-permute-start.31 = (bf16[2,32,1152]{2,1,0:T(8,128)(2,1)S(1)}, bf16[2,32,1152]{2,1,0:T(8,128)(2,1)S(1)}, u32[]{:S(2)}, u32[]{:S(2)}) collective-permute-start(bf16[2,32,1152]{2,1,0:T(8,128)(2,1)S(1)} %get-tuple-element.199), channel_id=1, source_target_pairs={{0,3},{1,2},{2,1},{3,0},{4,7},{5,6},{6,5},{7,4},{8,11},{9,10},{10,... | collective-permute-start | bytes 442376 | tf_op jit(solution)/shard_map/ppermute | solution.py:1209
  (27 other events, 179.2 us)
Sparse Core Ops, SparseCore 0:
  9.6 47.3 all-gather.4
  65.9 64.4 all-gather.6
  224.8 80.1 reduce-scatter.2
  326.4 55.4 reduce-scatter.4
where the time goes:
time: 417 us; the launch traced here: 409 us
  Pallas kernels  210 us (50%)
  waiting for transfers between devices  98.4 us (24%)
  starting transfers between devices  59.3 us (14%)
  between operations  14.5 us (3%)
  other arithmetic  14.2 us (3%)
  local copies, waits for them, and re-layouts  12.2 us (3%)
    pallas_call x1, Pallas kernels, attend_back(): pl.pallas_call(functools.partial(attend_back_kernel, span, (len(grads), l...  73.2 us
    pallas_call x2, Pallas kernels, feed(): pl.pallas_call(functools.partial(feed_kernel, len(kept)), grid_spec=pltpu...  49.3 us
    ppermute x16, waiting for transfers between devices, move(): return lax.ppermute(array, ALL, table(step, back))  48.2 us
    ppermute x16, starting transfers between devices, move(): return lax.ppermute(array, ALL, table(step, back))  44.5 us
    pallas_call x2, Pallas kernels, attend(): pl.pallas_call(functools.partial(attend_kernel, span), grid=(tiles,), in_...  38.9 us
    ppermute x6, waiting for transfers between devices, to_sum(): lax.ppermute(sent, axis, [(at, at ^ step) for at in range(size)])  28.1 us
    pallas_call x1, Pallas kernels, weight_grads(): pl.pallas_call(functools.partial(weight_grad_kernel, len(parts)), grid=(1...  19.5 us
    ppermute x6, waiting for transfers between devices, others(): lax.ppermute(array, axis, [(at, at ^ step) for at in range(size)])  12.6 us
  transfers between devices with their start and end apart: 37, of which 15 were waited for; matrix products, arithmetic and copies ran while one was open for 4% of the time, Pallas kernels for 51%

commit v1 on v0

--- a/solution.py
+++ b/solution.py
@@ -1186,10 +1186,10 @@
     grads = attend_back(qkv, list(early) + list(late), outs, auxes, info, 512, 1024)
 
     own, far = tokens_grads(which, grads, gathered, half)
+    second_grads, own, far = lax.optimization_barrier((second_grads, own, far))
+    second_grads = lax.psum_scatter(second_grads, "blk", scatter_dimension=0)
     summed = (own.astype(f32) + other_core(far).astype(f32)).astype(bf16)
     moved = [move(summed[step * half : (step + 1) * half], step, True) for step in range(n_blk)]
-    second_grads, summed = lax.optimization_barrier((second_grads, summed))
-    second_grads = lax.psum_scatter(second_grads, "blk", scatter_dimension=0)
     first_grads = own_grads(
         which,
         [after(item, summed) for item in grads],
@@ -1200,7 +1200,6 @@
         devices,
         half,
     )
-    first_grads, moved[0] = lax.optimization_barrier((first_grads, moved[0]))
 
     def to_sum(array, axis, me, size):
         terms = [lax.dynamic_index_in_dim(array, me, 0, keepdims=False)]
@@ -1217,7 +1216,7 @@
 
     first_grads = first_grads.reshape(n_pair, n_core, n_blk, share + 8, 3 * cols)
     total = add(to_sum(first_grads, "pair", pair, n_pair))
-    moved[1:], total = lax.optimization_barrier((moved[1:], total))
+    moved, total, second_grads = lax.optimization_barrier((moved, total, second_grads))
     terms = to_sum(jnp.moveaxis(total, 1, 0), "blk", blk, n_blk)
     returned = []
     for part in range(parts):

time: 417 us -> 412 us (0.988)
  waiting for transfers between devices: 98.4 us -> 92.7 us
    ppermute x16, waiting for transfers between devices: 48.2 us -> 40.4 us  [move(): return lax.ppermute(array, ALL, table(step, back))]
  transfers between devices with their start and end apart: 37 -> 37, of which waited for: 15 -> 16; matrix products, arithmetic and copies ran while one was open for 4% -> 4% of each run, Pallas kernels for 51% -> 52%
where the time goes in v1:
time: 412 us; the launch traced here: 404 us
  Pallas kernels  210 us (51%)
  waiting for transfers between devices  92.7 us (22%)
  starting transfers between devices  56.9 us (14%)
  other arithmetic  15.4 us (4%)
  between operations  14.7 us (4%)
  local copies, waits for them, and re-layouts  13.9 us (3%)
    pallas_call x1, Pallas kernels, attend_back(): pl.pallas_call(functools.partial(attend_back_kernel, span, (len(grads), l...  73.2 us
    pallas_call x2, Pallas kernels, feed(): pl.pallas_call(functools.partial(feed_kernel, len(kept)), grid_spec=pltpu...  49.3 us
    ppermute x16, starting transfers between devices, move(): return lax.ppermute(array, ALL, table(step, back))  42.1 us
    ppermute x16, waiting for transfers between devices, move(): return lax.ppermute(array, ALL, table(step, back))  40.4 us
    pallas_call x2, Pallas kernels, attend(): pl.pallas_call(functools.partial(attend_kernel, span), grid=(tiles,), in_...  38.8 us
    ppermute x6, waiting for transfers between devices, to_sum(): lax.ppermute(sent, axis, [(at, at ^ step) for at in range(size)])  30.5 us
    pallas_call x1, Pallas kernels, weight_grads(): pl.pallas_call(functools.partial(weight_grad_kernel, len(parts)), grid=(1...  19.5 us
    ppermute x6, waiting for transfers between devices, others(): lax.ppermute(array, axis, [(at, at ^ step) for at in range(size)])  12.6 us
  transfers between devices with their start and end apart: 37, of which 16 were waited for; matrix products, arithmetic and copies ran while one was open for 4% of the time, Pallas kernels for 52%

profile of v1, /device:TPU:9, one launch (start us, length us, event | category | flops | bytes accessed | tf_op | source)
XLA Modules:
  0.0 403.9 jit_solution(14861928457731128934)
XLA Ops:
  7.3 2.2 pack.1
  15.8 7.3 %collective-permute-done.2 = bf16[2,80,384]{2,1,0:T(8,128)(2,1)S(1)} collective-permute-done((bf16[2,80,384]{2,1,0:T(8,128)(2,1)S(1)}, bf16[2,80,384]{2,1,0:T(8,128)(2,1)S(1)}, u32[]{:S(2)}, u32[]{:S(2)}) %collective-permute-start.2) | collective-permute-done | bytes 122912 | tf_op jit(solution)/shard_map/ppermute | solution.py:1111
  23.1 5.3 %collective-permute-done.3 = bf16[2,80,384]{2,1,0:T(8,128)(2,1)S(1)} collective-permute-done((bf16[2,80,384]{2,1,0:T(8,128)(2,1)S(1)}, bf16[2,80,384]{2,1,0:T(8,128)(2,1)S(1)}, u32[]{:S(2)}, u32[]{:S(2)}) %collective-permute-start.3) | collective-permute-done | bytes 122912 | tf_op jit(solution)/shard_map/ppermute | solution.py:1111
  32.4 3.9 collective-permute-start.8
  36.3 6.3 %collective-permute-start.9 = (bf16[256,768]{1,0:T(8,128)(2,1)}, bf16[256,768]{1,0:T(8,128)(2,1)S(1)}, u32[]{:S(2)}, u32[]{:S(2)}) collective-permute-start(bf16[256,768]{1,0:T(8,128)(2,1)} %get-tuple-element.188), channel_id=1, source_target_pairs={{0,4},{1,0},{2,5},{3,1},{4,6},{5,2},{6,7},{7,3},{8,12},{9,8},{10,1... | collective-permute-start | bytes 1179656 | tf_op jit(solution)/shard_map/ppermute | solution.py:1087
  42.6 16.1 %collective-permute-done.8 = bf16[256,768]{1,0:T(8,128)(2,1)S(1)} collective-permute-done((bf16[256,768]{1,0:T(8,128)(2,1)}, bf16[256,768]{1,0:T(8,128)(2,1)S(1)}, u32[]{:S(2)}, u32[]{:S(2)}) %collective-permute-start.8) | collective-permute-done | bytes 393248 | tf_op jit(solution)/shard_map/ppermute | solution.py:1087
  58.7 4.7 %collective-permute-done.9 = bf16[256,768]{1,0:T(8,128)(2,1)S(1)} collective-permute-done((bf16[256,768]{1,0:T(8,128)(2,1)}, bf16[256,768]{1,0:T(8,128)(2,1)S(1)}, u32[]{:S(2)}, u32[]{:S(2)}) %collective-permute-start.9) | collective-permute-done | bytes 393248 | tf_op jit(solution)/shard_map/ppermute | solution.py:1087
  65.4 1.9 collective-permute-start.11
  67.4 3.1 collective-permute-start.10
  73.5 4.0 collective-permute-done.11
  77.5 3.1 collective-permute-done.10
  82.8 2.4 collective-permute-done.12.other_ref
  86.5 8.9 %project.1.query_ref.key_ref.value_ref = bf16[2048,1152]{1,0:T(8,128)(2,1)} custom-call(s32[1]{0:T(128)} %bitcast.10.core_ref, bf16[1024,768]{1,0:T(8,128)(2,1)} %copy-done, bf16[1024,768]{1,0:T(8,128)(2,1)} %copy-done.9, bf16[4,4,2,80,384]{4,3,2,1,0:T(8,128)(2,1)} %pad_maximum_fusion.1.gathered_ref.small_ref), custom_call_target="tpu_custom_call" | custom-call | flops 3623878656 | bytes 15728640 | tf_op jit(solution)/shard_map/project/pallas_call | solution.py:652
  95.4 19.4 %attend.2 = (bf16[512,384]{1,0:T(8,128)(2,1)}, bf16[512,384]{1,0:T(8,128)(2,1)}, f32[1024,384]{1,0:T(8,128)}, bf16[1024,384]{1,0:T(8,128)(2,1)}) custom-call(s32[9]{0:T(128)} %stack.103.info_ref, bf16[2048,1152]{1,0:T(8,128)(2,1)} %project.1.query_ref.key_ref.value_ref, bf16[2048,1152]{1,0:T(8,128)(2,1)} %project.1.query_ref.key_ref.value_ref, ...), custom_call_target="tpu_custom_call" | custom-call | flops 12884901888 | bytes 9437184 | tf_op jit(solution)/shard_map/attend/pallas_call | solution.py:382
  114.8 3.7 collective-permute-start.15
  118.5 3.8 collective-permute-start.16
  122.3 19.4 %attend.3 = (bf16[512,384]{1,0:T(8,128)(2,1)}, bf16[512,384]{1,0:T(8,128)(2,1)}, f32[1024,384]{1,0:T(8,128)}, bf16[1024,384]{1,0:T(8,128)(2,1)}) custom-call(s32[9]{0:T(128)} %stack.103.info_ref, bf16[2048,1152]{1,0:T(8,128)(2,1)} %project.1.query_ref.key_ref.value_ref, bf16[2048,1152]{1,0:T(8,128)(2,1)} %project.1.query_ref.key_ref.value_ref, ...), custom_call_target="tpu_custom_call" | custom-call | flops 12884901888 | bytes 9437184 | tf_op jit(solution)/shard_map/attend/pallas_call | solution.py:382
  141.6 3.7 collective-permute-start.14
  146.2 24.7 %feed.2 = (bf16[2,512,768]{2,1,0:T(8,128)(2,1)}, bf16[512,3072]{1,0:T(8,128)(2,1)}, bf16[512,768]{1,0:T(8,128)(2,1)}, bf16[512,3072]{1,0:T(8,128)(2,1)}, bf16[51...) custom-call(s32[2]{0:T(128)} %get-tuple-element.228.index_ref, ...), custom_call_target="tpu_custom_call" | custom-call | flops 10871635968 | bytes 24772608 | tf_op jit(solution)/shard_map/feed/pallas_call | solution.py:814
  175.4 24.7 %feed.3 = (bf16[2,512,768]{2,1,0:T(8,128)(2,1)}, bf16[512,3072]{1,0:T(8,128)(2,1)}, bf16[512,768]{1,0:T(8,128)(2,1)}, bf16[512,3072]{1,0:T(8,128)(2,1)}, bf16[51...) custom-call(s32[2]{0:T(128)} %get-tuple-element.227.index_ref, ...), custom_call_target="tpu_custom_call", output_to_operand_aliasing={{0}: (7, {})} | custom-call | flops 10871635968 | bytes 24772608 | tf_op jit(solution)/shard_map/feed/pallas_call | solution.py:814
  201.5 4.0 collective-permute-start.18
  205.6 19.5 %weight_grads.1 = bf16[32,9,24,768]{3,2,1,0:T(8,128)(2,1)} custom-call(bf16[512,3072]{1,0:T(8,128)(2,1)} %get-tuple-element.135.refs_0_, bf16[512,3072]{1,0:T(8,128)(2,1)} %get-tuple-element.136.refs_1_, bf16[512,768]{1,0:T(8,128)(2,1)} %get-tuple-element.121.refs_2_, bf16[512,768]{1,0:T(8,128)(2,1)} %get-tuple-element.137.refs_3_, ...), custom_call_target="tpu_custom_call" | custom-call | flops 10871635968 | bytes 24772608 | tf_op jit(solution)/shard_map/weight_grads/pallas_call | solution.py:927
  226.2 73.2 %attend_back.1 = (bf16[2048,384]{1,0:T(8,128)(2,1)}, bf16[2048,384]{1,0:T(8,128)(2,1)}, bf16[2048,384]{1,0:T(8,128)(2,1)}) custom-call(s32[9]{0:T(128)} %stack.103.info_ref, bf16[2048,1152]{1,0:T(8,128)(2,1)} %project.1.query_ref.key_ref.value_ref, bf16[2048,1152]{1,0:T(8,128)(2,1)} %project.1.query_ref.key_ref.value_ref, ...), custom_call_target="tpu_custom_call" | custom-call | flops 64424509440 | bytes 17301504 | tf_op jit(solution)/shard_map/attend_back/pallas_call | solution.py:487
  299.4 8.8 %tokens_grads.1 = (bf16[1024,768]{1,0:T(8,128)(2,1)}, bf16[1024,768]{1,0:T(8,128)(2,1)}) custom-call(s32[1]{0:T(128)} %bitcast.10.core_ref, bf16[2048,384]{1,0:T(8,128)(2,1)} %get-tuple-element.155.query_ref, bf16[2048,384]{1,0:T(8,128)(2,1)} %get-tuple-element.156.key_ref, bf16[2048,384]{1,0:T(8,128)(2,1)} %get-tuple-element.157.value_ref, ...), custom_call_target="tpu_custom_call" | custom-call | flops 3623878656 | bytes 9437184 | tf_op jit(solution)/shard_map/tokens_grads/pallas_call | solution.py:1026
  308.3 3.6 collective-permute-done.21
  313.6 9.6 %own_grads.1 = bf16[32,32,1152]{2,1,0:T(8,128)(2,1)} custom-call(s32[1]{0:T(128)} %bitcast.10.core_ref, bf16[2048,384]{1,0:T(8,128)(2,1)} %get-tuple-element.155.query_ref, bf16[2048,384]{1,0:T(8,128)(2,1)} %get-tuple-element.156.key_ref, bf16[2048,384]{1,0:T(8,128)(2,1)} %get-tuple-element.157.value_ref, bf16[1024,768]{1,0:T(8,128)(2,1)} %copy-done, ...), custom_call_target="tpu_custom_call" | custom-call | flops 3623878656 | bytes 9437184 | tf_op jit(solution)/shard_map/own_grads/pallas_call | solution.py:985
  323.2 2.6 dynamic-slice_bitcast_fusion.2
  328.6 3.2 collective-permute-start.22
  331.9 9.9 %collective-permute-done.28 = bf16[2,4,32,1152]{3,2,1,0:T(8,128)(2,1)S(1)} collective-permute-done((bf16[2,4,32,1152]{3,2,1,0:T(8,128)(2,1)}, bf16[2,4,32,1152]{3,2,1,0:T(8,128)(2,1)S(1)}, u32[]{:S(2)}, u32[]{:S(2)}) %collective-permute-start.28) | collective-permute-done | bytes 589856 | tf_op jit(solution)/shard_map/ppermute | solution.py:1208
  343.3 11.7 %collective-permute-done.27 = bf16[2,4,32,1152]{3,2,1,0:T(8,128)(2,1)S(1)} collective-permute-done((bf16[2,4,32,1152]{3,2,1,0:T(8,128)(2,1)}, bf16[2,4,32,1152]{3,2,1,0:T(8,128)(2,1)S(1)}, u32[]{:S(2)}, u32[]{:S(2)}) %collective-permute-start.27) | collective-permute-done | bytes 589856 | tf_op jit(solution)/shard_map/ppermute | solution.py:1208
  358.5 12.5 %collective-permute-done.23 = bf16[256,768]{1,0:T(8,128)(2,1)S(1)} collective-permute-done((bf16[256,768]{1,0:T(8,128)(2,1)S(1)}, bf16[256,768]{1,0:T(8,128)(2,1)S(1)}, u32[]{:S(2)}, u32[]{:S(2)}) %collective-permute-start.23) | collective-permute-done | bytes 393248 | tf_op jit(solution)/shard_map/ppermute | solution.py:1087
  382.5 8.5 %collective-permute-done.31 = bf16[2,32,1152]{2,1,0:T(8,128)(2,1)S(1)} collective-permute-done((bf16[2,32,1152]{2,1,0:T(8,128)(2,1)S(1)}, bf16[2,32,1152]{2,1,0:T(8,128)(2,1)S(1)}, u32[]{:S(2)}, u32[]{:S(2)}) %collective-permute-start.31) | collective-permute-done | bytes 147488 | tf_op jit(solution)/shard_map/ppermute | solution.py:1208
  (136 shorter events, 53.6 us)
Async XLA Ops:
  7.2 58.1 %all-gather.5.cloned.1.call-start = ((), (), s32[]{:S(2)}) async-start(), calls=%async_computation.4 | async-start | bytes 1658880 | tf_op jit(solution)/shard_map/all_gather | solution.py:1125
  9.5 135.9 %all-gather.7.cloned.1.call-start = ((), (), s32[]{:S(2)}) async-start(), calls=%async_computation.5 | async-start | bytes 11943936 | tf_op jit(solution)/shard_map/all_gather | solution.py:1135
  12.2 10.9 %collective-permute-start.2 = (bf16[2,80,384]{2,1,0:T(8,128)(2,1)S(1)}, bf16[2,80,384]{2,1,0:T(8,128)(2,1)S(1)}, u32[]{:S(2)}, u32[]{:S(2)}) collective-permute-start(bf16[2,80,384]{2,1,0:T(8,128)(2,1)S(1)} %pad_maximum_fusion.7), channel_id=1, source_target_pairs={{0,3},{1,2},{2,1},{3,0},{4,7},{5,6},{6,5},{7,4},{8,11},{9,10},{10,... | collective-permute-start | bytes 368648 | tf_op jit(solution)/shard_map/ppermute | solution.py:1111
  13.6 14.8 %collective-permute-start.3 = (bf16[2,80,384]{2,1,0:T(8,128)(2,1)S(1)}, bf16[2,80,384]{2,1,0:T(8,128)(2,1)S(1)}, u32[]{:S(2)}, u32[]{:S(2)}) collective-permute-start(bf16[2,80,384]{2,1,0:T(8,128)(2,1)S(1)} %pad_maximum_fusion.7), channel_id=1, source_target_pairs={{0,2},{1,3},{2,0},{3,1},{4,6},{5,7},{6,4},{7,5},{8,10},{9,11},{10,... | collective-permute-start | bytes 368648 | tf_op jit(solution)/shard_map/ppermute | solution.py:1111
  14.7 13.7 %collective-permute-start.4 = (bf16[2,80,384]{2,1,0:T(8,128)(2,1)S(1)}, bf16[2,80,384]{2,1,0:T(8,128)(2,1)S(1)}, u32[]{:S(2)}, u32[]{:S(2)}) collective-permute-start(bf16[2,80,384]{2,1,0:T(8,128)(2,1)S(1)} %pad_maximum_fusion.7), channel_id=1, source_target_pairs={{0,1},{1,0},{2,3},{3,2},{4,5},{5,4},{6,7},{7,6},{8,9},{9,8},{10,11... | collective-permute-start | bytes 368648 | tf_op jit(solution)/shard_map/ppermute | solution.py:1111
  28.6 34.9 %collective-permute-start.5 = (bf16[4,2,80,384]{3,2,1,0:T(8,128)(2,1)S(1)}, bf16[4,2,80,384]{3,2,1,0:T(8,128)(2,1)S(1)}, u32[]{:S(2)}, u32[]{:S(2)}) collective-permute-start(bf16[4,2,80,384]{3,2,1,0:T(8,128)(2,1)S(1)} %pad_maximum_fusion.5), channel_id=1, source_target_pairs={{0,8},{8,0},{16,24},{24,16},{1,9},{9,1},{17,25},{25,17},{2,10},{10... | collective-permute-start | bytes 1474568 | tf_op jit(solution)/shard_map/ppermute | solution.py:1111
  29.8 33.6 %collective-permute-start.6 = (bf16[4,2,80,384]{3,2,1,0:T(8,128)(2,1)S(1)}, bf16[4,2,80,384]{3,2,1,0:T(8,128)(2,1)S(1)}, u32[]{:S(2)}, u32[]{:S(2)}) collective-permute-start(bf16[4,2,80,384]{3,2,1,0:T(8,128)(2,1)S(1)} %pad_maximum_fusion.5), channel_id=1, source_target_pairs={{0,16},{8,24},{16,0},{24,8},{1,17},{9,25},{17,1},{25,9},{2,18},{10... | collective-permute-start | bytes 1474568 | tf_op jit(solution)/shard_map/ppermute | solution.py:1111
  31.1 32.4 %collective-permute-start.7 = (bf16[4,2,80,384]{3,2,1,0:T(8,128)(2,1)S(1)}, bf16[4,2,80,384]{3,2,1,0:T(8,128)(2,1)S(1)}, u32[]{:S(2)}, u32[]{:S(2)}) collective-permute-start(bf16[4,2,80,384]{3,2,1,0:T(8,128)(2,1)S(1)} %pad_maximum_fusion.5), channel_id=1, source_target_pairs={{0,24},{8,16},{16,8},{24,0},{1,25},{9,17},{17,9},{25,1},{2,26},{10... | collective-permute-start | bytes 1474568 | tf_op jit(solution)/shard_map/ppermute | solution.py:1111
  32.4 26.3 %collective-permute-start.8 = (bf16[256,768]{1,0:T(8,128)(2,1)}, bf16[256,768]{1,0:T(8,128)(2,1)S(1)}, u32[]{:S(2)}, u32[]{:S(2)}) collective-permute-start(bf16[256,768]{1,0:T(8,128)(2,1)} %get-tuple-element.191), channel_id=1, source_target_pairs={{0,0},{1,4},{2,1},{3,5},{4,2},{5,6},{6,3},{7,7},{8,8},{9,12},{10,9... | collective-permute-start | bytes 1179656 | tf_op jit(solution)/shard_map/ppermute | solution.py:1087
  36.3 27.1 %collective-permute-start.9 = (bf16[256,768]{1,0:T(8,128)(2,1)}, bf16[256,768]{1,0:T(8,128)(2,1)S(1)}, u32[]{:S(2)}, u32[]{:S(2)}) collective-permute-start(bf16[256,768]{1,0:T(8,128)(2,1)} %get-tuple-element.188), channel_id=1, source_target_pairs={{0,4},{1,0},{2,5},{3,1},{4,6},{5,2},{6,7},{7,3},{8,12},{9,8},{10,1... | collective-permute-start | bytes 1179656 | tf_op jit(solution)/shard_map/ppermute | solution.py:1087
  65.4 242.9 %reduce-scatter.3.cloned.1.call-start = ((), (), s32[]{:S(2)}) async-start(), calls=%async_computation.2 | async-start | bytes 11943936 | tf_op jit(solution)/shard_map/reduce_scatter | solution.py:1179
  65.4 12.1 %collective-permute-start.11 = (bf16[256,768]{1,0:T(8,128)(2,1)S(1)}, bf16[256,768]{1,0:T(8,128)(2,1)S(1)}, u32[]{:S(2)}, u32[]{:S(2)}) collective-permute-start(bf16[256,768]{1,0:T(8,128)(2,1)S(1)} %copy-done.7), channel_id=1, source_target_pairs={{0,5},{1,1},{2,4},{3,0},{4,7},{5,3},{6,6},{7,2},{8,13},{9,9},{10,1... | collective-permute-start | bytes 1179656 | tf_op jit(solution)/shard_map/ppermute | solution.py:1087
  67.4 13.2 %collective-permute-start.10 = (bf16[256,768]{1,0:T(8,128)(2,1)S(1)}, bf16[256,768]{1,0:T(8,128)(2,1)S(1)}, u32[]{:S(2)}, u32[]{:S(2)}) collective-permute-start(bf16[256,768]{1,0:T(8,128)(2,1)S(1)} %copy-done.6), channel_id=1, source_target_pairs={{0,1},{1,5},{2,0},{3,4},{4,3},{5,7},{6,2},{7,6},{8,9},{9,13},{10,8... | collective-permute-start | bytes 1179656 | tf_op jit(solution)/shard_map/ppermute | solution.py:1087
  114.8 30.6 %collective-permute-start.15 = (bf16[512,384]{1,0:T(8,128)(2,1)}, bf16[512,384]{1,0:T(8,128)(2,1)S(1)}, u32[]{:S(2)}, u32[]{:S(2)}) collective-permute-start(bf16[512,384]{1,0:T(8,128)(2,1)} %get-tuple-element.106), channel_id=1, source_target_pairs={{0,0},{4,1},{1,2},{5,3},{2,4},{6,5},{3,6},{7,7},{8,8},{12,9},{9,10... | collective-permute-start | bytes 1179656 | tf_op jit(solution)/shard_map/ppermute | solution.py:1087
  118.5 26.9 %collective-permute-start.16 = (bf16[512,384]{1,0:T(8,128)(2,1)}, bf16[512,384]{1,0:T(8,128)(2,1)S(1)}, u32[]{:S(2)}, u32[]{:S(2)}) collective-permute-start(bf16[512,384]{1,0:T(8,128)(2,1)} %get-tuple-element.107), channel_id=1, source_target_pairs={{4,0},{0,1},{5,2},{1,3},{6,4},{2,5},{7,6},{3,7},{12,8},{8,9},{13,1... | collective-permute-start | bytes 1179656 | tf_op jit(solution)/shard_map/ppermute | solution.py:1087
  141.6 32.8 %collective-permute-start.13 = (bf16[512,384]{1,0:T(8,128)(2,1)}, bf16[512,384]{1,0:T(8,128)(2,1)S(1)}, u32[]{:S(2)}, u32[]{:S(2)}) collective-permute-start(bf16[512,384]{1,0:T(8,128)(2,1)} %get-tuple-element.111), channel_id=1, source_target_pairs={{1,0},{5,1},{0,2},{4,3},{3,4},{7,5},{2,6},{6,7},{9,8},{13,9},{8,10... | collective-permute-start | bytes 1179656 | tf_op jit(solution)/shard_map/ppermute | solution.py:1087
  141.6 32.8 %collective-permute-start.14 = (bf16[512,384]{1,0:T(8,128)(2,1)}, bf16[512,384]{1,0:T(8,128)(2,1)S(1)}, u32[]{:S(2)}, u32[]{:S(2)}) collective-permute-start(bf16[512,384]{1,0:T(8,128)(2,1)} %get-tuple-element.112), channel_id=1, source_target_pairs={{5,0},{1,1},{4,2},{0,3},{7,4},{3,5},{6,6},{2,7},{13,8},{9,9},{12,1... | collective-permute-start | bytes 1179656 | tf_op jit(solution)/shard_map/ppermute | solution.py:1087
  170.9 34.6 %collective-permute-start.19 = (bf16[512,384]{1,0:T(8,128)(2,1)}, bf16[512,384]{1,0:T(8,128)(2,1)S(1)}, u32[]{:S(2)}, u32[]{:S(2)}) collective-permute-start(bf16[512,384]{1,0:T(8,128)(2,1)} %get-tuple-element.127), channel_id=1, source_target_pairs={{0,0},{1,4},{2,1},{3,5},{4,2},{5,6},{6,3},{7,7},{8,8},{9,12},{10,9... | collective-permute-start | bytes 1179656 | tf_op jit(solution)/shard_map/ppermute | solution.py:1087
  172.8 32.7 %collective-permute-start.20 = (bf16[512,384]{1,0:T(8,128)(2,1)}, bf16[512,384]{1,0:T(8,128)(2,1)S(1)}, u32[]{:S(2)}, u32[]{:S(2)}) collective-permute-start(bf16[512,384]{1,0:T(8,128)(2,1)} %get-tuple-element.128), channel_id=1, source_target_pairs={{0,4},{1,0},{2,5},{3,1},{4,6},{5,2},{6,7},{7,3},{8,12},{9,8},{10,1... | collective-permute-start | bytes 1179656 | tf_op jit(solution)/shard_map/ppermute | solution.py:1087
  200.0 25.0 %collective-permute-start.17 = (bf16[512,384]{1,0:T(8,128)(2,1)}, bf16[512,384]{1,0:T(8,128)(2,1)S(1)}, u32[]{:S(2)}, u32[]{:S(2)}) collective-permute-start(bf16[512,384]{1,0:T(8,128)(2,1)} %get-tuple-element.133), channel_id=1, source_target_pairs={{0,1},{1,5},{2,0},{3,4},{4,3},{5,7},{6,2},{7,6},{8,9},{9,13},{10,8... | collective-permute-start | bytes 1179656 | tf_op jit(solution)/shard_map/ppermute | solution.py:1087
  201.5 23.6 %collective-permute-start.18 = (bf16[512,384]{1,0:T(8,128)(2,1)}, bf16[512,384]{1,0:T(8,128)(2,1)S(1)}, u32[]{:S(2)}, u32[]{:S(2)}) collective-permute-start(bf16[512,384]{1,0:T(8,128)(2,1)} %get-tuple-element.134), channel_id=1, source_target_pairs={{0,5},{1,1},{2,4},{3,0},{4,7},{5,3},{6,6},{7,2},{8,13},{9,9},{10,1... | collective-permute-start | bytes 1179656 | tf_op jit(solution)/shard_map/ppermute | solution.py:1087
  226.0 145.8 %reduce-scatter.5.cloned.1.call-start = ((), (), s32[]{:S(2)}) async-start(), calls=%async_computation.3 | async-start | bytes 1658880 | tf_op jit(solution)/shard_map/reduce_scatter | solution.py:1190
  325.9 15.9 %collective-permute-start.28 = (bf16[2,4,32,1152]{3,2,1,0:T(8,128)(2,1)}, bf16[2,4,32,1152]{3,2,1,0:T(8,128)(2,1)S(1)}, u32[]{:S(2)}, u32[]{:S(2)}) collective-permute-start(bf16[2,4,32,1152]{3,2,1,0:T(8,128)(2,1)} %get-tuple-element.178), channel_id=1, source_target_pairs={{0,24},{8,16},{16,8},{24,0},{1,25},{9,17},{17,9},{25,1},{2,26},{10... | collective-permute-start | bytes 1769480 | tf_op jit(solution)/shard_map/ppermute | solution.py:1208
  327.0 28.0 %collective-permute-start.27 = (bf16[2,4,32,1152]{3,2,1,0:T(8,128)(2,1)}, bf16[2,4,32,1152]{3,2,1,0:T(8,128)(2,1)S(1)}, u32[]{:S(2)}, u32[]{:S(2)}) collective-permute-start(bf16[2,4,32,1152]{3,2,1,0:T(8,128)(2,1)} %get-tuple-element.179), channel_id=1, source_target_pairs={{0,16},{8,24},{16,0},{24,8},{1,17},{9,25},{17,1},{25,9},{2,18},{10... | collective-permute-start | bytes 1769480 | tf_op jit(solution)/shard_map/ppermute | solution.py:1208
  328.1 28.8 %collective-permute-start.26 = (bf16[2,4,32,1152]{3,2,1,0:T(8,128)(2,1)S(1)}, bf16[2,4,32,1152]{3,2,1,0:T(8,128)(2,1)}, u32[]{:S(2)}, u32[]{:S(2)}) collective-permute-start(bf16[2,4,32,1152]{3,2,1,0:T(8,128)(2,1)S(1)} %get-tuple-element.177), channel_id=1, source_target_pairs={{0,8},{8,0},{16,24},{24,16},{1,9},{9,1},{17,25},{25,17},{2,10},{10... | collective-permute-start | bytes 1769480 | tf_op jit(solution)/shard_map/ppermute | solution.py:1208
  328.6 29.8 %collective-permute-start.22 = (bf16[256,768]{1,0:T(8,128)(2,1)S(1)}, bf16[256,768]{1,0:T(8,128)(2,1)S(1)}, u32[]{:S(2)}, u32[]{:S(2)}) collective-permute-start(bf16[256,768]{1,0:T(8,128)(2,1)S(1)} %get-tuple-element.187), channel_id=1, source_target_pairs={{0,0},{4,1},{1,2},{5,3},{2,4},{6,5},{3,6},{7,7},{8,8},{12,9},{9,10... | collective-permute-start | bytes 1179656 | tf_op jit(solution)/shard_map/ppermute | solution.py:1087
  331.8 39.2 %collective-permute-start.23 = (bf16[256,768]{1,0:T(8,128)(2,1)S(1)}, bf16[256,768]{1,0:T(8,128)(2,1)S(1)}, u32[]{:S(2)}, u32[]{:S(2)}) collective-permute-start(bf16[256,768]{1,0:T(8,128)(2,1)S(1)} %get-tuple-element.186), channel_id=1, source_target_pairs={{4,0},{0,1},{5,2},{1,3},{6,4},{2,5},{7,6},{3,7},{12,8},{8,9},{13,1... | collective-permute-start | bytes 1179656 | tf_op jit(solution)/shard_map/ppermute | solution.py:1087
  341.8 29.2 %collective-permute-start.24 = (bf16[256,768]{1,0:T(8,128)(2,1)S(1)}, bf16[256,768]{1,0:T(8,128)(2,1)S(1)}, u32[]{:S(2)}, u32[]{:S(2)}) collective-permute-start(bf16[256,768]{1,0:T(8,128)(2,1)S(1)} %get-tuple-element.185), channel_id=1, source_target_pairs={{1,0},{5,1},{0,2},{4,3},{3,4},{7,5},{2,6},{6,7},{9,8},{13,9},{8,10... | collective-permute-start | bytes 1179656 | tf_op jit(solution)/shard_map/ppermute | solution.py:1087
  355.0 16.8 %collective-permute-start.25 = (bf16[256,768]{1,0:T(8,128)(2,1)S(1)}, bf16[256,768]{1,0:T(8,128)(2,1)}, u32[]{:S(2)}, u32[]{:S(2)}) collective-permute-start(bf16[256,768]{1,0:T(8,128)(2,1)S(1)} %get-tuple-element.184), channel_id=1, source_target_pairs={{5,0},{1,1},{4,2},{0,3},{7,4},{3,5},{6,6},{2,7},{13,8},{9,9},{12,1... | collective-permute-start | bytes 1179656 | tf_op jit(solution)/shard_map/ppermute | solution.py:1087
  374.5 7.6 %collective-permute-start.29 = (bf16[2,32,1152]{2,1,0:T(8,128)(2,1)S(1)}, bf16[2,32,1152]{2,1,0:T(8,128)(2,1)S(1)}, u32[]{:S(2)}, u32[]{:S(2)}) collective-permute-start(bf16[2,32,1152]{2,1,0:T(8,128)(2,1)S(1)} %get-tuple-element.203), channel_id=1, source_target_pairs={{0,1},{1,0},{2,3},{3,2},{4,5},{5,4},{6,7},{7,6},{8,9},{9,8},{10,11... | collective-permute-start | bytes 442376 | tf_op jit(solution)/shard_map/ppermute | solution.py:1208
  375.7 6.8 %collective-permute-start.30 = (bf16[2,32,1152]{2,1,0:T(8,128)(2,1)S(1)}, bf16[2,32,1152]{2,1,0:T(8,128)(2,1)S(1)}, u32[]{:S(2)}, u32[]{:S(2)}) collective-permute-start(bf16[2,32,1152]{2,1,0:T(8,128)(2,1)S(1)} %get-tuple-element.202), channel_id=1, source_target_pairs={{0,2},{1,3},{2,0},{3,1},{4,6},{5,7},{6,4},{7,5},{8,10},{9,11},{10,... | collective-permute-start | bytes 442376 | tf_op jit(solution)/shard_map/ppermute | solution.py:1208
  375.7 15.3 %collective-permute-start.31 = (bf16[2,32,1152]{2,1,0:T(8,128)(2,1)S(1)}, bf16[2,32,1152]{2,1,0:T(8,128)(2,1)S(1)}, u32[]{:S(2)}, u32[]{:S(2)}) collective-permute-start(bf16[2,32,1152]{2,1,0:T(8,128)(2,1)S(1)} %get-tuple-element.201), channel_id=1, source_target_pairs={{0,3},{1,2},{2,1},{3,0},{4,7},{5,6},{6,5},{7,4},{8,11},{9,10},{10,... | collective-permute-start | bytes 442376 | tf_op jit(solution)/shard_map/ppermute | solution.py:1208
  (23 other events, 106.5 us)
Sparse Core Ops, SparseCore 0:
  9.6 47.3 all-gather.4
  65.5 64.4 all-gather.6
  225.3 80.3 reduce-scatter.2
  308.4 30.4 reduce-scatter.4

commit v2 on v1

--- a/solution.py
+++ b/solution.py
@@ -1245,14 +1245,17 @@
         for at in range(0, 3 * cols, cols)
     ]
     lines = (kept[share + 1 :].astype(f32) + crossed[share + 1 :].astype(f32)).reshape(-1)
-    own_lines = own_part(lines[: 6 * width].reshape(6, width), share)
+    biases = [projections[at][share : share + 1] for at in (0, 2)]
+    own_lines = own_part(
+        jnp.concatenate(biases + [lines[: 6 * width].reshape(6, width)], axis=0), share
+    )
     up_line = own_part(lines[6 * width : (6 + fold) * width], fold * share)
     return (
         (layer_out, tokens_grad)
         + tuple(item[:share] for item in projections)
         + late
-        + (own_part(projections[0][share], share), own_part(projections[2][share], share))
-        + (own_lines[0], up_line, own_lines[1], own_lines[2], own_lines[3], own_lines[4], own_lines[5])
+        + (own_lines[0], own_lines[1], own_lines[2], up_line)
+        + tuple(own_lines[at] for at in range(3, 8))
     )
 
 

time: 412 us -> 411 us (level)
  no operation moved by 1% of the time
where the time goes in v2:
time: 411 us; the launch traced here: 403 us
  Pallas kernels  210 us (51%)
  waiting for transfers between devices  92.7 us (23%)
  starting transfers between devices  56.9 us (14%)
  between operations  14.7 us (4%)
  other arithmetic  14.3 us (3%)
  local copies, waits for them, and re-layouts  13.8 us (3%)
    pallas_call x1, Pallas kernels, attend_back(): pl.pallas_call(functools.partial(attend_back_kernel, span, (len(grads), l...  73.2 us
    pallas_call x2, Pallas kernels, feed(): pl.pallas_call(functools.partial(feed_kernel, len(kept)), grid_spec=pltpu...  49.3 us
    ppermute x16, starting transfers between devices, move(): return lax.ppermute(array, ALL, table(step, back))  42.1 us
    ppermute x16, waiting for transfers between devices, move(): return lax.ppermute(array, ALL, table(step, back))  40.4 us
    pallas_call x2, Pallas kernels, attend(): pl.pallas_call(functools.partial(attend_kernel, span), grid=(tiles,), in_...  38.8 us
    ppermute x6, waiting for transfers between devices, to_sum(): lax.ppermute(sent, axis, [(at, at ^ step) for at in range(size)])  30.5 us
    pallas_call x1, Pallas kernels, weight_grads(): pl.pallas_call(functools.partial(weight_grad_kernel, len(parts)), grid=(1...  19.5 us
    ppermute x6, waiting for transfers between devices, others(): lax.ppermute(array, axis, [(at, at ^ step) for at in range(size)])  12.6 us
  transfers between devices with their start and end apart: 37, of which 16 were waited for; matrix products, arithmetic and copies ran while one was open for 4% of the time, Pallas kernels for 52%

profile of v2, /device:TPU:9, one launch (start us, length us, event | category | flops | bytes accessed | tf_op | source)
XLA Modules:
  0.0 402.7 jit_solution(11011315541428886089)
XLA Ops:
  7.3 2.2 pack.1
  15.8 7.3 %collective-permute-done.2 = bf16[2,80,384]{2,1,0:T(8,128)(2,1)S(1)} collective-permute-done((bf16[2,80,384]{2,1,0:T(8,128)(2,1)S(1)}, bf16[2,80,384]{2,1,0:T(8,128)(2,1)S(1)}, u32[]{:S(2)}, u32[]{:S(2)}) %collective-permute-start.2) | collective-permute-done | bytes 122912 | tf_op jit(solution)/shard_map/ppermute | solution.py:1111
  23.1 5.3 %collective-permute-done.3 = bf16[2,80,384]{2,1,0:T(8,128)(2,1)S(1)} collective-permute-done((bf16[2,80,384]{2,1,0:T(8,128)(2,1)S(1)}, bf16[2,80,384]{2,1,0:T(8,128)(2,1)S(1)}, u32[]{:S(2)}, u32[]{:S(2)}) %collective-permute-start.3) | collective-permute-done | bytes 122912 | tf_op jit(solution)/shard_map/ppermute | solution.py:1111
  32.4 3.9 collective-permute-start.8
  36.3 6.3 %collective-permute-start.9 = (bf16[256,768]{1,0:T(8,128)(2,1)}, bf16[256,768]{1,0:T(8,128)(2,1)S(1)}, u32[]{:S(2)}, u32[]{:S(2)}) collective-permute-start(bf16[256,768]{1,0:T(8,128)(2,1)} %get-tuple-element.188), channel_id=1, source_target_pairs={{0,4},{1,0},{2,5},{3,1},{4,6},{5,2},{6,7},{7,3},{8,12},{9,8},{10,1... | collective-permute-start | bytes 1179656 | tf_op jit(solution)/shard_map/ppermute | solution.py:1087
  42.6 16.1 %collective-permute-done.8 = bf16[256,768]{1,0:T(8,128)(2,1)S(1)} collective-permute-done((bf16[256,768]{1,0:T(8,128)(2,1)}, bf16[256,768]{1,0:T(8,128)(2,1)S(1)}, u32[]{:S(2)}, u32[]{:S(2)}) %collective-permute-start.8) | collective-permute-done | bytes 393248 | tf_op jit(solution)/shard_map/ppermute | solution.py:1087
  58.7 4.7 %collective-permute-done.9 = bf16[256,768]{1,0:T(8,128)(2,1)S(1)} collective-permute-done((bf16[256,768]{1,0:T(8,128)(2,1)}, bf16[256,768]{1,0:T(8,128)(2,1)S(1)}, u32[]{:S(2)}, u32[]{:S(2)}) %collective-permute-start.9) | collective-permute-done | bytes 393248 | tf_op jit(solution)/shard_map/ppermute | solution.py:1087
  65.4 1.9 collective-permute-start.11
  67.4 3.1 collective-permute-start.10
  73.5 4.0 collective-permute-done.11
  77.5 3.1 collective-permute-done.10
  82.8 2.4 collective-permute-done.12.other_ref
  86.5 8.9 %project.1.query_ref.key_ref.value_ref = bf16[2048,1152]{1,0:T(8,128)(2,1)} custom-call(s32[1]{0:T(128)} %bitcast.10.core_ref, bf16[1024,768]{1,0:T(8,128)(2,1)} %copy-done, bf16[1024,768]{1,0:T(8,128)(2,1)} %copy-done.9, bf16[4,4,2,80,384]{4,3,2,1,0:T(8,128)(2,1)} %pad_maximum_fusion.1.gathered_ref.small_ref), custom_call_target="tpu_custom_call" | custom-call | flops 3623878656 | bytes 15728640 | tf_op jit(solution)/shard_map/project/pallas_call | solution.py:652
  95.4 19.4 %attend.2 = (bf16[512,384]{1,0:T(8,128)(2,1)}, bf16[512,384]{1,0:T(8,128)(2,1)}, f32[1024,384]{1,0:T(8,128)}, bf16[1024,384]{1,0:T(8,128)(2,1)}) custom-call(s32[9]{0:T(128)} %stack.103.info_ref, bf16[2048,1152]{1,0:T(8,128)(2,1)} %project.1.query_ref.key_ref.value_ref, bf16[2048,1152]{1,0:T(8,128)(2,1)} %project.1.query_ref.key_ref.value_ref, ...), custom_call_target="tpu_custom_call" | custom-call | flops 12884901888 | bytes 9437184 | tf_op jit(solution)/shard_map/attend/pallas_call | solution.py:382
  114.8 3.7 collective-permute-start.15
  118.5 3.8 collective-permute-start.16
  122.3 19.4 %attend.3 = (bf16[512,384]{1,0:T(8,128)(2,1)}, bf16[512,384]{1,0:T(8,128)(2,1)}, f32[1024,384]{1,0:T(8,128)}, bf16[1024,384]{1,0:T(8,128)(2,1)}) custom-call(s32[9]{0:T(128)} %stack.103.info_ref, bf16[2048,1152]{1,0:T(8,128)(2,1)} %project.1.query_ref.key_ref.value_ref, bf16[2048,1152]{1,0:T(8,128)(2,1)} %project.1.query_ref.key_ref.value_ref, ...), custom_call_target="tpu_custom_call" | custom-call | flops 12884901888 | bytes 9437184 | tf_op jit(solution)/shard_map/attend/pallas_call | solution.py:382
  141.6 3.7 collective-permute-start.14
  146.2 24.7 %feed.2 = (bf16[2,512,768]{2,1,0:T(8,128)(2,1)}, bf16[512,3072]{1,0:T(8,128)(2,1)}, bf16[512,768]{1,0:T(8,128)(2,1)}, bf16[512,3072]{1,0:T(8,128)(2,1)}, bf16[51...) custom-call(s32[2]{0:T(128)} %get-tuple-element.230.index_ref, ...), custom_call_target="tpu_custom_call" | custom-call | flops 10871635968 | bytes 24772608 | tf_op jit(solution)/shard_map/feed/pallas_call | solution.py:814
  175.4 24.7 %feed.3 = (bf16[2,512,768]{2,1,0:T(8,128)(2,1)}, bf16[512,3072]{1,0:T(8,128)(2,1)}, bf16[512,768]{1,0:T(8,128)(2,1)}, bf16[512,3072]{1,0:T(8,128)(2,1)}, bf16[51...) custom-call(s32[2]{0:T(128)} %get-tuple-element.229.index_ref, ...), custom_call_target="tpu_custom_call", output_to_operand_aliasing={{0}: (7, {})} | custom-call | flops 10871635968 | bytes 24772608 | tf_op jit(solution)/shard_map/feed/pallas_call | solution.py:814
  201.5 4.0 %collective-permute-start.18 = (bf16[512,384]{1,0:T(8,128)(2,1)}, bf16[512,384]{1,0:T(8,128)(2,1)S(1)}, u32[]{:S(2)}, u32[]{:S(2)}) collective-permute-start(bf16[512,384]{1,0:T(8,128)(2,1)} %get-tuple-element.134), channel_id=1, source_target_pairs={{0,5},{1,1},{2,4},{3,0},{4,7},{5,3},{6,6},{7,2},{8,13},{9,9},{10,1... | collective-permute-start | bytes 1179656 | tf_op jit(solution)/shard_map/ppermute | solution.py:1087
  205.6 19.5 %weight_grads.1 = bf16[32,9,24,768]{3,2,1,0:T(8,128)(2,1)} custom-call(bf16[512,3072]{1,0:T(8,128)(2,1)} %get-tuple-element.135.refs_0_, bf16[512,3072]{1,0:T(8,128)(2,1)} %get-tuple-element.136.refs_1_, bf16[512,768]{1,0:T(8,128)(2,1)} %get-tuple-element.121.refs_2_, bf16[512,768]{1,0:T(8,128)(2,1)} %get-tuple-element.137.refs_3_, ...), custom_call_target="tpu_custom_call" | custom-call | flops 10871635968 | bytes 24772608 | tf_op jit(solution)/shard_map/weight_grads/pallas_call | solution.py:927
  226.2 73.2 %attend_back.1 = (bf16[2048,384]{1,0:T(8,128)(2,1)}, bf16[2048,384]{1,0:T(8,128)(2,1)}, bf16[2048,384]{1,0:T(8,128)(2,1)}) custom-call(s32[9]{0:T(128)} %stack.103.info_ref, bf16[2048,1152]{1,0:T(8,128)(2,1)} %project.1.query_ref.key_ref.value_ref, bf16[2048,1152]{1,0:T(8,128)(2,1)} %project.1.query_ref.key_ref.value_ref, ...), custom_call_target="tpu_custom_call" | custom-call | flops 64424509440 | bytes 17301504 | tf_op jit(solution)/shard_map/attend_back/pallas_call | solution.py:487
  299.4 8.8 %tokens_grads.1 = (bf16[1024,768]{1,0:T(8,128)(2,1)}, bf16[1024,768]{1,0:T(8,128)(2,1)}) custom-call(s32[1]{0:T(128)} %bitcast.10.core_ref, bf16[2048,384]{1,0:T(8,128)(2,1)} %get-tuple-element.155.query_ref, bf16[2048,384]{1,0:T(8,128)(2,1)} %get-tuple-element.156.key_ref, bf16[2048,384]{1,0:T(8,128)(2,1)} %get-tuple-element.157.value_ref, ...), custom_call_target="tpu_custom_call" | custom-call | flops 3623878656 | bytes 9437184 | tf_op jit(solution)/shard_map/tokens_grads/pallas_call | solution.py:1026
  308.3 3.6 collective-permute-done.21
  313.6 9.6 %own_grads.1 = bf16[32,32,1152]{2,1,0:T(8,128)(2,1)} custom-call(s32[1]{0:T(128)} %bitcast.10.core_ref, bf16[2048,384]{1,0:T(8,128)(2,1)} %get-tuple-element.155.query_ref, bf16[2048,384]{1,0:T(8,128)(2,1)} %get-tuple-element.156.key_ref, bf16[2048,384]{1,0:T(8,128)(2,1)} %get-tuple-element.157.value_ref, bf16[1024,768]{1,0:T(8,128)(2,1)} %copy-done, ...), custom_call_target="tpu_custom_call" | custom-call | flops 3623878656 | bytes 9437184 | tf_op jit(solution)/shard_map/own_grads/pallas_call | solution.py:985
  323.2 2.6 dynamic-slice_bitcast_fusion.2
  328.6 3.2 collective-permute-start.22
  331.9 9.9 %collective-permute-done.28 = bf16[2,4,32,1152]{3,2,1,0:T(8,128)(2,1)S(1)} collective-permute-done((bf16[2,4,32,1152]{3,2,1,0:T(8,128)(2,1)}, bf16[2,4,32,1152]{3,2,1,0:T(8,128)(2,1)S(1)}, u32[]{:S(2)}, u32[]{:S(2)}) %collective-permute-start.28) | collective-permute-done | bytes 589856 | tf_op jit(solution)/shard_map/ppermute | solution.py:1208
  343.3 11.7 %collective-permute-done.27 = bf16[2,4,32,1152]{3,2,1,0:T(8,128)(2,1)S(1)} collective-permute-done((bf16[2,4,32,1152]{3,2,1,0:T(8,128)(2,1)}, bf16[2,4,32,1152]{3,2,1,0:T(8,128)(2,1)S(1)}, u32[]{:S(2)}, u32[]{:S(2)}) %collective-permute-start.27) | collective-permute-done | bytes 589856 | tf_op jit(solution)/shard_map/ppermute | solution.py:1208
  358.5 12.5 %collective-permute-done.23 = bf16[256,768]{1,0:T(8,128)(2,1)S(1)} collective-permute-done((bf16[256,768]{1,0:T(8,128)(2,1)S(1)}, bf16[256,768]{1,0:T(8,128)(2,1)S(1)}, u32[]{:S(2)}, u32[]{:S(2)}) %collective-permute-start.23) | collective-permute-done | bytes 393248 | tf_op jit(solution)/shard_map/ppermute | solution.py:1087
  382.5 8.5 %collective-permute-done.31 = bf16[2,32,1152]{2,1,0:T(8,128)(2,1)S(1)} collective-permute-done((bf16[2,32,1152]{2,1,0:T(8,128)(2,1)S(1)}, bf16[2,32,1152]{2,1,0:T(8,128)(2,1)S(1)}, u32[]{:S(2)}, u32[]{:S(2)}) %collective-permute-start.31) | collective-permute-done | bytes 147488 | tf_op jit(solution)/shard_map/ppermute | solution.py:1208
  (134 shorter events, 52.5 us)
Async XLA Ops:
  7.2 58.1 %all-gather.5.cloned.1.call-start = ((), (), s32[]{:S(2)}) async-start(), calls=%async_computation.4 | async-start | bytes 1658880 | tf_op jit(solution)/shard_map/all_gather | solution.py:1125
  9.5 135.9 %all-gather.7.cloned.1.call-start = ((), (), s32[]{:S(2)}) async-start(), calls=%async_computation.5 | async-start | bytes 11943936 | tf_op jit(solution)/shard_map/all_gather | solution.py:1135
  12.2 10.9 %collective-permute-start.2 = (bf16[2,80,384]{2,1,0:T(8,128)(2,1)S(1)}, bf16[2,80,384]{2,1,0:T(8,128)(2,1)S(1)}, u32[]{:S(2)}, u32[]{:S(2)}) collective-permute-start(bf16[2,80,384]{2,1,0:T(8,128)(2,1)S(1)} %pad_maximum_fusion.7), channel_id=1, source_target_pairs={{0,3},{1,2},{2,1},{3,0},{4,7},{5,6},{6,5},{7,4},{8,11},{9,10},{10,... | collective-permute-start | bytes 368648 | tf_op jit(solution)/shard_map/ppermute | solution.py:1111
  13.6 14.8 %collective-permute-start.3 = (bf16[2,80,384]{2,1,0:T(8,128)(2,1)S(1)}, bf16[2,80,384]{2,1,0:T(8,128)(2,1)S(1)}, u32[]{:S(2)}, u32[]{:S(2)}) collective-permute-start(bf16[2,80,384]{2,1,0:T(8,128)(2,1)S(1)} %pad_maximum_fusion.7), channel_id=1, source_target_pairs={{0,2},{1,3},{2,0},{3,1},{4,6},{5,7},{6,4},{7,5},{8,10},{9,11},{10,... | collective-permute-start | bytes 368648 | tf_op jit(solution)/shard_map/ppermute | solution.py:1111
  14.7 13.7 %collective-permute-start.4 = (bf16[2,80,384]{2,1,0:T(8,128)(2,1)S(1)}, bf16[2,80,384]{2,1,0:T(8,128)(2,1)S(1)}, u32[]{:S(2)}, u32[]{:S(2)}) collective-permute-start(bf16[2,80,384]{2,1,0:T(8,128)(2,1)S(1)} %pad_maximum_fusion.7), channel_id=1, source_target_pairs={{0,1},{1,0},{2,3},{3,2},{4,5},{5,4},{6,7},{7,6},{8,9},{9,8},{10,11... | collective-permute-start | bytes 368648 | tf_op jit(solution)/shard_map/ppermute | solution.py:1111
  28.6 34.9 %collective-permute-start.5 = (bf16[4,2,80,384]{3,2,1,0:T(8,128)(2,1)S(1)}, bf16[4,2,80,384]{3,2,1,0:T(8,128)(2,1)S(1)}, u32[]{:S(2)}, u32[]{:S(2)}) collective-permute-start(bf16[4,2,80,384]{3,2,1,0:T(8,128)(2,1)S(1)} %pad_maximum_fusion.5), channel_id=1, source_target_pairs={{0,8},{8,0},{16,24},{24,16},{1,9},{9,1},{17,25},{25,17},{2,10},{10... | collective-permute-start | bytes 1474568 | tf_op jit(solution)/shard_map/ppermute | solution.py:1111
  29.8 33.6 %collective-permute-start.6 = (bf16[4,2,80,384]{3,2,1,0:T(8,128)(2,1)S(1)}, bf16[4,2,80,384]{3,2,1,0:T(8,128)(2,1)S(1)}, u32[]{:S(2)}, u32[]{:S(2)}) collective-permute-start(bf16[4,2,80,384]{3,2,1,0:T(8,128)(2,1)S(1)} %pad_maximum_fusion.5), channel_id=1, source_target_pairs={{0,16},{8,24},{16,0},{24,8},{1,17},{9,25},{17,1},{25,9},{2,18},{10... | collective-permute-start | bytes 1474568 | tf_op jit(solution)/shard_map/ppermute | solution.py:1111
  31.1 32.4 %collective-permute-start.7 = (bf16[4,2,80,384]{3,2,1,0:T(8,128)(2,1)S(1)}, bf16[4,2,80,384]{3,2,1,0:T(8,128)(2,1)S(1)}, u32[]{:S(2)}, u32[]{:S(2)}) collective-permute-start(bf16[4,2,80,384]{3,2,1,0:T(8,128)(2,1)S(1)} %pad_maximum_fusion.5), channel_id=1, source_target_pairs={{0,24},{8,16},{16,8},{24,0},{1,25},{9,17},{17,9},{25,1},{2,26},{10... | collective-permute-start | bytes 1474568 | tf_op jit(solution)/shard_map/ppermute | solution.py:1111
  32.4 26.3 %collective-permute-start.8 = (bf16[256,768]{1,0:T(8,128)(2,1)}, bf16[256,768]{1,0:T(8,128)(2,1)S(1)}, u32[]{:S(2)}, u32[]{:S(2)}) collective-permute-start(bf16[256,768]{1,0:T(8,128)(2,1)} %get-tuple-element.191), channel_id=1, source_target_pairs={{0,0},{1,4},{2,1},{3,5},{4,2},{5,6},{6,3},{7,7},{8,8},{9,12},{10,9... | collective-permute-start | bytes 1179656 | tf_op jit(solution)/shard_map/ppermute | solution.py:1087
  36.3 27.1 %collective-permute-start.9 = (bf16[256,768]{1,0:T(8,128)(2,1)}, bf16[256,768]{1,0:T(8,128)(2,1)S(1)}, u32[]{:S(2)}, u32[]{:S(2)}) collective-permute-start(bf16[256,768]{1,0:T(8,128)(2,1)} %get-tuple-element.188), channel_id=1, source_target_pairs={{0,4},{1,0},{2,5},{3,1},{4,6},{5,2},{6,7},{7,3},{8,12},{9,8},{10,1... | collective-permute-start | bytes 1179656 | tf_op jit(solution)/shard_map/ppermute | solution.py:1087
  65.4 242.9 %reduce-scatter.3.cloned.1.call-start = ((), (), s32[]{:S(2)}) async-start(), calls=%async_computation.2 | async-start | bytes 11943936 | tf_op jit(solution)/shard_map/reduce_scatter | solution.py:1179
  65.4 12.1 %collective-permute-start.11 = (bf16[256,768]{1,0:T(8,128)(2,1)S(1)}, bf16[256,768]{1,0:T(8,128)(2,1)S(1)}, u32[]{:S(2)}, u32[]{:S(2)}) collective-permute-start(bf16[256,768]{1,0:T(8,128)(2,1)S(1)} %copy-done.7), channel_id=1, source_target_pairs={{0,5},{1,1},{2,4},{3,0},{4,7},{5,3},{6,6},{7,2},{8,13},{9,9},{10,1... | collective-permute-start | bytes 1179656 | tf_op jit(solution)/shard_map/ppermute | solution.py:1087
  67.4 13.2 %collective-permute-start.10 = (bf16[256,768]{1,0:T(8,128)(2,1)S(1)}, bf16[256,768]{1,0:T(8,128)(2,1)S(1)}, u32[]{:S(2)}, u32[]{:S(2)}) collective-permute-start(bf16[256,768]{1,0:T(8,128)(2,1)S(1)} %copy-done.6), channel_id=1, source_target_pairs={{0,1},{1,5},{2,0},{3,4},{4,3},{5,7},{6,2},{7,6},{8,9},{9,13},{10,8... | collective-permute-start | bytes 1179656 | tf_op jit(solution)/shard_map/ppermute | solution.py:1087
  114.8 30.6 %collective-permute-start.15 = (bf16[512,384]{1,0:T(8,128)(2,1)}, bf16[512,384]{1,0:T(8,128)(2,1)S(1)}, u32[]{:S(2)}, u32[]{:S(2)}) collective-permute-start(bf16[512,384]{1,0:T(8,128)(2,1)} %get-tuple-element.106), channel_id=1, source_target_pairs={{0,0},{4,1},{1,2},{5,3},{2,4},{6,5},{3,6},{7,7},{8,8},{12,9},{9,10... | collective-permute-start | bytes 1179656 | tf_op jit(solution)/shard_map/ppermute | solution.py:1087
  118.5 26.9 %collective-permute-start.16 = (bf16[512,384]{1,0:T(8,128)(2,1)}, bf16[512,384]{1,0:T(8,128)(2,1)S(1)}, u32[]{:S(2)}, u32[]{:S(2)}) collective-permute-start(bf16[512,384]{1,0:T(8,128)(2,1)} %get-tuple-element.107), channel_id=1, source_target_pairs={{4,0},{0,1},{5,2},{1,3},{6,4},{2,5},{7,6},{3,7},{12,8},{8,9},{13,1... | collective-permute-start | bytes 1179656 | tf_op jit(solution)/shard_map/ppermute | solution.py:1087
  141.6 32.8 %collective-permute-start.13 = (bf16[512,384]{1,0:T(8,128)(2,1)}, bf16[512,384]{1,0:T(8,128)(2,1)S(1)}, u32[]{:S(2)}, u32[]{:S(2)}) collective-permute-start(bf16[512,384]{1,0:T(8,128)(2,1)} %get-tuple-element.111), channel_id=1, source_target_pairs={{1,0},{5,1},{0,2},{4,3},{3,4},{7,5},{2,6},{6,7},{9,8},{13,9},{8,10... | collective-permute-start | bytes 1179656 | tf_op jit(solution)/shard_map/ppermute | solution.py:1087
  141.6 32.8 %collective-permute-start.14 = (bf16[512,384]{1,0:T(8,128)(2,1)}, bf16[512,384]{1,0:T(8,128)(2,1)S(1)}, u32[]{:S(2)}, u32[]{:S(2)}) collective-permute-start(bf16[512,384]{1,0:T(8,128)(2,1)} %get-tuple-element.112), channel_id=1, source_target_pairs={{5,0},{1,1},{4,2},{0,3},{7,4},{3,5},{6,6},{2,7},{13,8},{9,9},{12,1... | collective-permute-start | bytes 1179656 | tf_op jit(solution)/shard_map/ppermute | solution.py:1087
  170.9 34.6 %collective-permute-start.19 = (bf16[512,384]{1,0:T(8,128)(2,1)}, bf16[512,384]{1,0:T(8,128)(2,1)S(1)}, u32[]{:S(2)}, u32[]{:S(2)}) collective-permute-start(bf16[512,384]{1,0:T(8,128)(2,1)} %get-tuple-element.127), channel_id=1, source_target_pairs={{0,0},{1,4},{2,1},{3,5},{4,2},{5,6},{6,3},{7,7},{8,8},{9,12},{10,9... | collective-permute-start | bytes 1179656 | tf_op jit(solution)/shard_map/ppermute | solution.py:1087
  172.8 32.7 %collective-permute-start.20 = (bf16[512,384]{1,0:T(8,128)(2,1)}, bf16[512,384]{1,0:T(8,128)(2,1)S(1)}, u32[]{:S(2)}, u32[]{:S(2)}) collective-permute-start(bf16[512,384]{1,0:T(8,128)(2,1)} %get-tuple-element.128), channel_id=1, source_target_pairs={{0,4},{1,0},{2,5},{3,1},{4,6},{5,2},{6,7},{7,3},{8,12},{9,8},{10,1... | collective-permute-start | bytes 1179656 | tf_op jit(solution)/shard_map/ppermute | solution.py:1087
  200.0 25.0 %collective-permute-start.17 = (bf16[512,384]{1,0:T(8,128)(2,1)}, bf16[512,384]{1,0:T(8,128)(2,1)S(1)}, u32[]{:S(2)}, u32[]{:S(2)}) collective-permute-start(bf16[512,384]{1,0:T(8,128)(2,1)} %get-tuple-element.133), channel_id=1, source_target_pairs={{0,1},{1,5},{2,0},{3,4},{4,3},{5,7},{6,2},{7,6},{8,9},{9,13},{10,8... | collective-permute-start | bytes 1179656 | tf_op jit(solution)/shard_map/ppermute | solution.py:1087
  201.5 23.6 %collective-permute-start.18 = (bf16[512,384]{1,0:T(8,128)(2,1)}, bf16[512,384]{1,0:T(8,128)(2,1)S(1)}, u32[]{:S(2)}, u32[]{:S(2)}) collective-permute-start(bf16[512,384]{1,0:T(8,128)(2,1)} %get-tuple-element.134), channel_id=1, source_target_pairs={{0,5},{1,1},{2,4},{3,0},{4,7},{5,3},{6,6},{7,2},{8,13},{9,9},{10,1... | collective-permute-start | bytes 1179656 | tf_op jit(solution)/shard_map/ppermute | solution.py:1087
  226.0 145.8 %reduce-scatter.5.cloned.1.call-start = ((), (), s32[]{:S(2)}) async-start(), calls=%async_computation.3 | async-start | bytes 1658880 | tf_op jit(solution)/shard_map/reduce_scatter | solution.py:1190
  325.9 15.9 %collective-permute-start.28 = (bf16[2,4,32,1152]{3,2,1,0:T(8,128)(2,1)}, bf16[2,4,32,1152]{3,2,1,0:T(8,128)(2,1)S(1)}, u32[]{:S(2)}, u32[]{:S(2)}) collective-permute-start(bf16[2,4,32,1152]{3,2,1,0:T(8,128)(2,1)} %get-tuple-element.178), channel_id=1, source_target_pairs={{0,24},{8,16},{16,8},{24,0},{1,25},{9,17},{17,9},{25,1},{2,26},{10... | collective-permute-start | bytes 1769480 | tf_op jit(solution)/shard_map/ppermute | solution.py:1208
  327.0 28.0 %collective-permute-start.27 = (bf16[2,4,32,1152]{3,2,1,0:T(8,128)(2,1)}, bf16[2,4,32,1152]{3,2,1,0:T(8,128)(2,1)S(1)}, u32[]{:S(2)}, u32[]{:S(2)}) collective-permute-start(bf16[2,4,32,1152]{3,2,1,0:T(8,128)(2,1)} %get-tuple-element.179), channel_id=1, source_target_pairs={{0,16},{8,24},{16,0},{24,8},{1,17},{9,25},{17,1},{25,9},{2,18},{10... | collective-permute-start | bytes 1769480 | tf_op jit(solution)/shard_map/ppermute | solution.py:1208
  328.1 28.8 %collective-permute-start.26 = (bf16[2,4,32,1152]{3,2,1,0:T(8,128)(2,1)S(1)}, bf16[2,4,32,1152]{3,2,1,0:T(8,128)(2,1)}, u32[]{:S(2)}, u32[]{:S(2)}) collective-permute-start(bf16[2,4,32,1152]{3,2,1,0:T(8,128)(2,1)S(1)} %get-tuple-element.177), channel_id=1, source_target_pairs={{0,8},{8,0},{16,24},{24,16},{1,9},{9,1},{17,25},{25,17},{2,10},{10... | collective-permute-start | bytes 1769480 | tf_op jit(solution)/shard_map/ppermute | solution.py:1208
  328.6 29.8 %collective-permute-start.22 = (bf16[256,768]{1,0:T(8,128)(2,1)S(1)}, bf16[256,768]{1,0:T(8,128)(2,1)S(1)}, u32[]{:S(2)}, u32[]{:S(2)}) collective-permute-start(bf16[256,768]{1,0:T(8,128)(2,1)S(1)} %get-tuple-element.187), channel_id=1, source_target_pairs={{0,0},{4,1},{1,2},{5,3},{2,4},{6,5},{3,6},{7,7},{8,8},{12,9},{9,10... | collective-permute-start | bytes 1179656 | tf_op jit(solution)/shard_map/ppermute | solution.py:1087
  331.8 39.2 %collective-permute-start.23 = (bf16[256,768]{1,0:T(8,128)(2,1)S(1)}, bf16[256,768]{1,0:T(8,128)(2,1)S(1)}, u32[]{:S(2)}, u32[]{:S(2)}) collective-permute-start(bf16[256,768]{1,0:T(8,128)(2,1)S(1)} %get-tuple-element.186), channel_id=1, source_target_pairs={{4,0},{0,1},{5,2},{1,3},{6,4},{2,5},{7,6},{3,7},{12,8},{8,9},{13,1... | collective-permute-start | bytes 1179656 | tf_op jit(solution)/shard_map/ppermute | solution.py:1087
  341.8 29.2 %collective-permute-start.24 = (bf16[256,768]{1,0:T(8,128)(2,1)S(1)}, bf16[256,768]{1,0:T(8,128)(2,1)S(1)}, u32[]{:S(2)}, u32[]{:S(2)}) collective-permute-start(bf16[256,768]{1,0:T(8,128)(2,1)S(1)} %get-tuple-element.185), channel_id=1, source_target_pairs={{1,0},{5,1},{0,2},{4,3},{3,4},{7,5},{2,6},{6,7},{9,8},{13,9},{8,10... | collective-permute-start | bytes 1179656 | tf_op jit(solution)/shard_map/ppermute | solution.py:1087
  355.0 16.8 %collective-permute-start.25 = (bf16[256,768]{1,0:T(8,128)(2,1)S(1)}, bf16[256,768]{1,0:T(8,128)(2,1)}, u32[]{:S(2)}, u32[]{:S(2)}) collective-permute-start(bf16[256,768]{1,0:T(8,128)(2,1)S(1)} %get-tuple-element.184), channel_id=1, source_target_pairs={{5,0},{1,1},{4,2},{0,3},{7,4},{3,5},{6,6},{2,7},{13,8},{9,9},{12,1... | collective-permute-start | bytes 1179656 | tf_op jit(solution)/shard_map/ppermute | solution.py:1087
  374.5 7.6 %collective-permute-start.29 = (bf16[2,32,1152]{2,1,0:T(8,128)(2,1)S(1)}, bf16[2,32,1152]{2,1,0:T(8,128)(2,1)S(1)}, u32[]{:S(2)}, u32[]{:S(2)}) collective-permute-start(bf16[2,32,1152]{2,1,0:T(8,128)(2,1)S(1)} %get-tuple-element.203), channel_id=1, source_target_pairs={{0,1},{1,0},{2,3},{3,2},{4,5},{5,4},{6,7},{7,6},{8,9},{9,8},{10,11... | collective-permute-start | bytes 442376 | tf_op jit(solution)/shard_map/ppermute | solution.py:1208
  375.7 6.8 %collective-permute-start.30 = (bf16[2,32,1152]{2,1,0:T(8,128)(2,1)S(1)}, bf16[2,32,1152]{2,1,0:T(8,128)(2,1)S(1)}, u32[]{:S(2)}, u32[]{:S(2)}) collective-permute-start(bf16[2,32,1152]{2,1,0:T(8,128)(2,1)S(1)} %get-tuple-element.202), channel_id=1, source_target_pairs={{0,2},{1,3},{2,0},{3,1},{4,6},{5,7},{6,4},{7,5},{8,10},{9,11},{10,... | collective-permute-start | bytes 442376 | tf_op jit(solution)/shard_map/ppermute | solution.py:1208
  375.7 15.3 %collective-permute-start.31 = (bf16[2,32,1152]{2,1,0:T(8,128)(2,1)S(1)}, bf16[2,32,1152]{2,1,0:T(8,128)(2,1)S(1)}, u32[]{:S(2)}, u32[]{:S(2)}) collective-permute-start(bf16[2,32,1152]{2,1,0:T(8,128)(2,1)S(1)} %get-tuple-element.201), channel_id=1, source_target_pairs={{0,3},{1,2},{2,1},{3,0},{4,7},{5,6},{6,5},{7,4},{8,11},{9,10},{10,... | collective-permute-start | bytes 442376 | tf_op jit(solution)/shard_map/ppermute | solution.py:1208
  (23 other events, 106.5 us)
Sparse Core Ops, SparseCore 0:
  9.6 47.3 all-gather.4
  65.5 64.4 all-gather.6
  225.3 80.3 reduce-scatter.2
  308.4 30.4 reduce-scatter.4
